TPU v7x, 256 devices: a whole 4x4x8 slice. The times are simulated.
256 devices in a mesh: atoms: 4 (over y), frames: 64 (over x, z, core).
Axes of the slice: x: 4, y: 4, z: 8, core: 2. Of those that a mesh axis runs over, the one named last changes fastest.
Arguments:
- frames: float32 [1536, 3, 98304], P('frames', None, 'atoms'), may hold values from -48 to 48
- mean_structure: float32 [3, 98304], P(None, 'atoms'), may hold values from -16 to 16
- atom_weight: float32 [98304], P('atoms'), may hold values from 1 to 32
- subspace: bfloat16 [32, 3, 98304], P(None, None, 'atoms'), may hold values from -6 to 6
Outputs:
- new_mean: float32 [3, 98304], P(None, ('atoms', 'frames'))
- image: float32 [32, 3, 98304], P(None, None, ('atoms', 'frames'))
- basis: float32 [32, 3, 98304], P(None, None, ('atoms', 'frames'))
All inputs are finite; a program needn't handle non-finite values.
Results may differ from a plain program's by a relative error of at most 0.0076.
Values may be sent and summed in bfloat16 or wider, within the bound.
A program may use at most 128 MiB of HBM per device.

v0:
```python
import jax
import jax.numpy as jnp
from jax import lax
from jax.sharding import PartitionSpec as P

A = 98304
NEWTON = 8


def newton_polar(moment):
    norm = jnp.sqrt(jnp.sum(moment * moment, axis=(1, 2)))
    x = moment / norm[:, None, None]
    for step in range(NEWTON):
        x00, x01, x02 = (x[:, 0, 0], x[:, 0, 1], x[:, 0, 2])
        x10, x11, x12 = (x[:, 1, 0], x[:, 1, 1], x[:, 1, 2])
        x20, x21, x22 = (x[:, 2, 0], x[:, 2, 1], x[:, 2, 2])
        c00 = x11 * x22 - x12 * x21
        c01 = x12 * x20 - x10 * x22
        c02 = x10 * x21 - x11 * x20
        c10 = x02 * x21 - x01 * x22
        c11 = x00 * x22 - x02 * x20
        c12 = x01 * x20 - x00 * x21
        c20 = x01 * x12 - x02 * x11
        c21 = x02 * x10 - x00 * x12
        c22 = x00 * x11 - x01 * x10
        determ = x00 * c00 + x01 * c01 + x02 * c02
        cofac = jnp.stack(
            [
                jnp.stack([c00, c01, c02], axis=1),
                jnp.stack([c10, c11, c12], axis=1),
                jnp.stack([c20, c21, c22], axis=1),
            ],
            axis=1,
        )
        x = 0.5 * (x + cofac / determ[:, None, None])
    return x


def per_device(frames, mean_structure, atom_weight, subspace):
    highest = lax.Precision.HIGHEST
    frame_count = frames.shape[0] * lax.axis_size("frames")
    weighted = atom_weight[None, :] * mean_structure
    local_first = jnp.einsum("a,fia->fi", atom_weight, frames, precision=highest)
    total, mean_sum = lax.psum((jnp.sum(atom_weight), jnp.sum(weighted, axis=1)), "atoms")
    mean_center = mean_sum / total
    centered = (mean_structure - mean_center[:, None]) * atom_weight[None, :]
    local_second = jnp.einsum("ia,fja->fij", centered, frames, precision=highest)
    first, second = lax.psum((local_first, local_second), "atoms")
    moment = second / total
    frame_center = first / total
    rotation = newton_polar(moment)
    anchor = mean_center[:, None] - mean_structure
    moved = jnp.einsum("fij,fja->fia", rotation, frames, precision=highest)
    offset = jnp.einsum("fij,fj->fi", rotation, frame_center, precision=highest)
    displaced = (moved - offset[:, :, None] + anchor[None]).astype(jnp.bfloat16)
    frame_rows = displaced.shape[0]
    vectors = subspace.shape[0]
    local_proj = jnp.einsum(
        "fc,kc->fk",
        displaced.reshape(frame_rows, -1),
        subspace.reshape(vectors, -1),
        preferred_element_type=jnp.float32,
    )
    projection = lax.psum(local_proj, "atoms")
    proj_total = lax.psum(jnp.sum(local_proj, axis=0), ("atoms", "frames"))
    centered_projection = (projection - proj_total / frame_count).astype(jnp.bfloat16)
    term = jnp.einsum(
        "fk,fia->kia", centered_projection, displaced, preferred_element_type=jnp.float32
    )
    shift_sum = jnp.sum(displaced, axis=0, dtype=jnp.float32)
    stacked = jnp.concatenate([term, shift_sum[None]], axis=0)
    reduced = lax.psum_scatter(stacked, "frames", scatter_dimension=2, tiled=True)
    image_sum = reduced[:vectors]
    mean_shift = reduced[vectors]
    image = image_sum / frame_count
    width = image.shape[2]
    own_mean = lax.dynamic_slice_in_dim(mean_structure, lax.axis_index("frames") * width, width, 1)
    new_mean = own_mean + mean_shift / frame_count
    flat = image.reshape(vectors, -1)
    gram = lax.psum(jnp.dot(flat, flat.T, precision=highest), ("atoms", "frames")) / (3 * A)
    lower = jnp.linalg.cholesky(gram)
    basis = jax.scipy.linalg.solve_triangular(lower, flat, lower=True)
    return (new_mean, image, basis.reshape(image.shape))


def solution(mesh):
    return jax.shard_map(
        per_device,
        mesh=mesh,
        in_specs=(P("frames", None, "atoms"), P(None, "atoms"), P("atoms"), P(None, None, "atoms")),
        out_specs=(
            P(None, ("atoms", "frames")),
            P(None, None, ("atoms", "frames")),
            P(None, None, ("atoms", "frames")),
        ),
        check_vma=False,
    )
```

profile of v0, /device:TPU:1, one launch (start us, length us, event | category | flops | bytes accessed | tf_op | source)
XLA Modules:
  0.0 459.7 jit_solution(17343104478468763775)
XLA Ops:
  7.2 1.3 multiply_reduce_fusion
  8.6 1.5 reduce_sum.46
  10.1 10.1 %all-reduce.1 = (f32[3]{0:T(128)S(1)}, f32[]{:T(128)}) all-reduce(f32[3]{0:T(128)S(1)} %multiply_reduce_fusion, f32[]{:T(128)} %reduce_sum.46), channel_id=1, replica_groups=mesh['atoms'=4,'frames'=64] {'atoms'}, use_global_device_ids=true, to_apply=%region_1.0 | all-reduce | flops 4 | bytes 32 | tf_op jit(solution)/shard_map/psum | solution.py:44
  20.2 0.8 broadcast_divide_fusion.2
  21.0 16.9 %convolution_bitcast_fusion.1 = f32[24,3,3]{0,1,2:T(4,128)S(1)} fusion(f32[24,3,24576]{2,0,1:T(8,128)} %param.4, f32[3,24576]{1,0:T(4,128)} %param.5, f32[3]{0:T(128)S(1)} %broadcast_divide_fusion.2, f32[24576]{0:T(1024)} %param.6), kind=kOutput, calls=%fused_computation.12 | convolution fusion | flops 63848448 | bytes 7471980 | tf_op jit(solution)/shard_map/ia,fja->fij/dot_general | solution.py:47
  38.0 13.8 %fusion.34 = f32[1,24,3]{1,0,2:T(1,128)S(1)} fusion(f32[24576,1,1]{0,1,2:T(1,128)S(1)} %bitcast.242, f32[24,3,24576]{2,0,1:T(8,128)S(1)} %copy-done), kind=kOutput, calls=%fused_computation.168 | convolution fusion | flops 21233664 | bytes 7176480 | tf_op jit(solution)/shard_map/a,fia->fi/dot_general | solution.py:43
  51.8 11.1 %all-reduce = (f32[24,3,3]{0,1,2:T(4,128)S(1)}, f32[24,3]{1,0:T(8,128)S(1)}) all-reduce(f32[24,3,3]{0,1,2:T(4,128)S(1)} %convolution_bitcast_fusion.1, f32[24,3]{1,0:T(8,128)S(1)} %bitcast.243), channel_id=1, replica_groups=mesh['atoms'=4,'frames'=64] {'atoms'}, use_global_device_ids=true, to_apply=%region_4.0 | all-reduce | flops 288 | bytes 2304 | tf_op jit(solution)/shard_map/psum | solution.py:48
  62.9 0.7 fusion.32
  63.6 0.7 sqrt_multiply_fusion
  65.5 0.1 broadcast_subtract_fusion
  65.8 0.1 copy.62
  65.9 0.7 broadcast_divide_fusion
  66.6 0.3 fusion.35
  66.9 29.3 %convert_reduce_fusion = (f32[3,24576]{1,0:T(4,128)S(1)}, bf16[24,3,24576]{2,1,0:T(4,128)(2,1)S(1)}) fusion(f32[3,24576]{1,0:T(4,128)S(1)} %broadcast_subtract_fusion, f32[24,3]{1,0:T(8,128)S(1)} %bitcast.269, f32[24,3,3]{2,1,0:T(4,128)S(1)} %copy.62, f32[24,3,24576]{2,0,1:T(8,128)} %param.4), kind=kOutput, calls=%fused_computation.5 | convolution fusion | flops 72474624 | bytes 11207808 | tf_op jit(solution)/shard_map/fij,fja->fia/dot_general | solution.py:53
  96.2 2.1 copy-done.1
  98.3 5.1 %fusion.33 = (f32[32]{0:T(128)S(1)}, f32[24,32]{1,0:T(8,128)S(1)}) fusion(bf16[32,3,24576]{2,0,1:T(8,128)(2,1)S(1)} %bitcast.241, bf16[24,3,24576]{2,1,0:T(4,128)(2,1)S(1)} %get-tuple-element.88), kind=kOutput, calls=%fused_computation.166 | convolution fusion | flops 113246944 | bytes 8260736 | tf_op jit(solution)/shard_map/fc,kc->fk/dot_general | solution.py:58
  103.5 12.2 %psum.53 = f32[24,32]{1,0:T(8,128)S(1)} all-reduce(f32[24,32]{1,0:T(8,128)S(1)} %get-tuple-element.90), channel_id=1, replica_groups=mesh['atoms'=4,'frames'=64] {'atoms'}, use_global_device_ids=true, to_apply=%region_7.0 | all-reduce | flops 768 | bytes 6144 | tf_op jit(solution)/shard_map/psum | solution.py:64
  115.7 87.8 %psum.54 = f32[32]{0:T(128)S(1)} all-reduce(f32[32]{0:T(128)S(1)} %get-tuple-element.89), channel_id=1, replica_groups=mesh['atoms'=4,'frames'=64] {'atoms','frames'}, use_global_device_ids=true, to_apply=%region_9.0 | all-reduce | flops 32 | bytes 256 | tf_op jit(solution)/shard_map/psum | solution.py:65
  203.4 0.2 broadcast_in_dim.3
  203.6 9.0 %fusion.3 = f32[32,3,24576]{2,0,1:T(8,128)S(1)} fusion(bf16[24,3,24576]{2,1,0:T(4,128)(2,1)} %copy-done.1, f32[24,32]{1,0:T(8,128)S(1)} %psum.53, f32[32]{0:T(128)S(1)} %broadcast_multiply_fusion.1), kind=kOutput, calls=%fused_computation.6 | convolution fusion | flops 113247744 | bytes 12979328 | tf_op jit(solution)/shard_map/fk,fia->kia/dot_general | solution.py:67
  212.6 5.7 %pad_maximum_fusion = f32[33,3,24576]{2,0,1:T(8,128)} fusion(f32[1,3,24576]{2,0,1:T(1,128)S(1)} %broadcast_in_dim.3, f32[32,3,24576]{2,0,1:T(8,128)S(1)} %fusion.3), kind=kLoop, calls=%fused_computation.3 | loop fusion | flops 2433024 | bytes 19464192 | tf_op jit(solution)/shard_map/concatenate | solution.py:71
  218.3 144.5 %reduce-scatter.2.cloned.1.call-done = f32[33,3,384]{2,0,1:T(8,128)} async-done(((f32[33,3,24576]{2,0,1:T(8,128)}), f32[33,3,384]{2,0,1:T(8,128)}) %reduce-scatter.2.cloned.1.call-update) | async-done | bytes 152080 | tf_op jit(solution)/shard_map/reduce_scatter | solution.py:72
  362.8 0.9 slice_multiply_fusion
  363.7 0.3 convolution_bitcast_fusion
  364.0 78.6 %psum.55 = f32[32,32]{0,1:T(8,128)S(1)} all-reduce(f32[32,32]{0,1:T(8,128)S(1)} %convolution_bitcast_fusion), channel_id=1, replica_groups=mesh['atoms'=4,'frames'=64] {'atoms','frames'}, use_global_device_ids=true, to_apply=%region_12.0 | all-reduce | flops 1024 | bytes 8192 | tf_op jit(solution)/shard_map/psum | solution.py:80
  442.7 2.9 cholesky.16
  445.6 0.6 compare_reduce_fusion
  446.3 0.7 fusion.18
  446.9 2.4 custom-call.7
  449.4 0.8 slice_multiply_fusion.1
  450.2 0.6 bitcast_add_fusion.1
  450.8 1.9 fusion.15
  (94 shorter events, 1.2 us)
Async XLA Ops:
  7.2 30.8 %copy-start.3 = (f32[24576]{0:T(1024)S(1)}, f32[24576]{0:T(1024)}, u32[]{:S(2)}) copy-start(f32[24576]{0:T(1024)} %param.6) | copy-start | bytes 294916
  7.2 355.6 %reduce-scatter.2.cloned.1.call-start = ((), (), s32[]{:S(2)}) async-start(), calls=%async_computation.1 | async-start | bytes 11980800 | tf_op jit(solution)/shard_map/reduce_scatter | solution.py:72
  20.2 17.7 %copy-start = (f32[24,3,24576]{2,0,1:T(8,128)S(1)}, f32[24,3,24576]{2,0,1:T(8,128)}, u32[]{:S(2)}) copy-start(f32[24,3,24576]{2,0,1:T(8,128)} %param.4) | copy-start | bytes 21233668
  21.0 44.4 %copy-start.2 = (f32[3,24576]{1,0:T(4,128)S(1)}, f32[3,24576]{1,0:T(4,128)}, u32[]{:S(2)}) copy-start(f32[3,24576]{1,0:T(4,128)} %param.5) | copy-start | bytes 884740
  65.5 32.9 %slice-start = ((s8[4718592]{0:T(1024)(128)(4,1)}), s8[524288]{0:T(1024)(128)(4,1)S(1)}, s32[]{:S(2)}) async-start(s8[4718592]{0:T(1024)(128)(4,1)} %bitcast.240), calls=%async_computation.2 | async-start | bytes 1048576
  66.9 31.5 %slice-start.1 = ((s8[4718592]{0:T(1024)(128)(4,1)}), s8[4194304]{0:T(1024)(128)(4,1)S(1)}, s32[]{:S(2)}) async-start(s8[4718592]{0:T(1024)(128)(4,1)} %bitcast.240), calls=%async_computation.3 | async-start | bytes 8388608
  96.2 2.1 copy-start.1
  363.7 89.0 %copy-start.4 = (f32[32,3,384]{2,0,1:T(8,128)}, f32[32,3,384]{2,0,1:T(8,128)S(1)}, u32[]{:S(2)}) copy-start(f32[32,3,384]{2,0,1:T(8,128)S(1)} %slice_multiply_fusion) | copy-start | bytes 442372
Sparse Core Ops, SparseCore 0:
  218.4 144.3 reduce-scatter.1
where the time goes:
time: 464 us; the launch traced here: 460 us
  blocking collectives  200 us (43%)
  waiting for transfers between devices  144 us (31%)
  matrix products  76.6 us (17%)
  other arithmetic  21.2 us (5%)
  between operations  14.9 us (3%)
    reduce_scatter x1, waiting for transfers between devices, per_device(): lax.psum_scatter(stacked, 'frames', scatter_dimension=2, tiled=True)  144 us
    psum x1, blocking collectives, per_device(): proj_total = lax.psum(jnp.sum(local_proj, axis=0), ('atoms', 'frames'))  87.8 us
    psum x1, blocking collectives, per_device(): lax.psum(jnp.dot(flat, flat.T, precision=highest), ('atoms', 'frames'))  78.6 us
    dot_general x1, matrix products, per_device(): moved = jnp.einsum('fij,fja->fia', rotation, frames, precision=highest)  29.3 us
    dot_general x1, matrix products, per_device(): jnp.einsum('ia,fja->fij', centered, frames, precision=highest)  16.9 us
    dot_general x1, matrix products, per_device(): jnp.einsum('a,fia->fi', atom_weight, frames, precision=highest)  13.8 us
    psum x1, blocking collectives, per_device(): projection = lax.psum(local_proj, 'atoms')  12.2 us
    psum x1, blocking collectives, per_device(): first, second = lax.psum((local_first, local_second), 'atoms')  11.1 us
  transfers between devices with their start and end apart: 1, of which 1 were waited for; matrix products, arithmetic and copies ran while one was open for 0% of the time, Pallas kernels for 0%

commit v1 on v0

v1 whole, which is shorter than its diff:
```python
import jax
import jax.numpy as jnp
from jax import lax
from jax.experimental import pallas as pl
from jax.experimental.pallas import tpu as pltpu
from jax.sharding import PartitionSpec as P

ATOMS = 98304
FRAMES = 1536
NEWTON = 8
NX, NZ, NC, NY = 4, 8, 2, 4
NF = 24
FP = 32
K = 32
AL = ATOMS // NY
BLK = AL // (NX * NZ * NC)
NB = NX * NZ
CHUNKS = 8
CW = AL // CHUNKS
STEP = 512
F32 = jnp.float32
BF16 = jnp.bfloat16
MESH = pl.DeviceIdType.MESH
HIGHEST = lax.Precision.HIGHEST
STREAMS = tuple((h, d) for h in (0, 1) for d in (1, -1))
NT = (((1,), (1,)), ((), ()))


def steps_of(n, half, direction):
    return n // 2 if (direction == 1) == (half == 0) else n // 2 - 1


def newton(m):
    norm = m[0] * m[0]
    for e in m[1:]:
        norm = norm + e * e
    inv = 1.0 / jnp.sqrt(norm)
    x = [e * inv for e in m]
    for _ in range(NEWTON):
        x00, x01, x02, x10, x11, x12, x20, x21, x22 = x
        cof = [
            x11 * x22 - x12 * x21,
            x12 * x20 - x10 * x22,
            x10 * x21 - x11 * x20,
            x02 * x21 - x01 * x22,
            x00 * x22 - x02 * x20,
            x01 * x20 - x00 * x21,
            x01 * x12 - x02 * x11,
            x02 * x10 - x00 * x12,
            x00 * x11 - x01 * x10,
        ]
        det = x00 * cof[0] + x01 * cof[1] + x02 * cof[2]
        r = 1.0 / det
        x = [0.5 * (a + c * r) for a, c in zip(x, cof)]
    return x


def kernel(
    x_hbm, ms_ref, w_ref, s_hbm, nm_ref, img_ref, bas_ref,
    xv, sv, dall, dsend, rot, ex1, ex2, pp, gsq, pbx, pbz, cpt, gx, gy, gz,
    a1s, a1r, b1s, b1r, a2s, a2r, b2s, b2r, acca, accb,
    xsem, ssem, y1s, y1r, y2s, y2r, px_s, px_r, pz_s, pz_r, pp_s, pp_r, dx_s, dx_r,
    gx_s, gx_r, gy_s, gy_r, gz_s, gz_r, a1ss, a1rs, b1ss, b1rs, a2ss, a2rs, b2ss, b2rs,
):
    y = lax.axis_index("atoms")
    n = lax.axis_index("frames")
    px = n // (NZ * NC)
    pz = (n // NC) % NZ
    pc = n % NC

    def dev(dx=0, dz=0, dc=0, dy=0):
        tx = (px + (dx + NX)) % NX
        tz = (pz + (dz + NZ)) % NZ
        tc = (pc + dc) % NC
        return ((y + dy) % NY, (tx * NZ + tz) * NC + tc)

    y_peers = [dev(dy=j) for j in range(1, NY)]
    xc_peers = [dev(dx=j // 2, dc=j % 2) for j in range(1, NX * NC)]
    z_peers = [dev(dz=j) for j in range(1, NZ)]
    partner = dev(dc=1)

    loads = []
    for q in range(CHUNKS):
        cols = pl.ds(q * CW, CW)
        cp = pltpu.make_async_copy(x_hbm.at[:, :, cols], xv.at[:, :, cols], xsem.at[q])
        cp.start()
        loads.append(cp)
    sload = pltpu.make_async_copy(s_hbm, sv, ssem)
    sload.start()

    barrier = pltpu.get_barrier_semaphore()
    for peer in y_peers + xc_peers + z_peers:
        pl.semaphore_signal(barrier, inc=1, device_id=peer, device_id_type=MESH)

    def remote(src, dst, ssm, rsm, peer):
        return pltpu.make_async_remote_copy(
            src_ref=src, dst_ref=dst, send_sem=ssm, recv_sem=rsm, device_id=peer, device_id_type=MESH
        )

    pending = []

    def exchange(buf, peers, ssm, rsm):
        copies = []
        for j, peer in enumerate(peers):
            copies.append(remote(buf.at[0], buf.at[j + 1], ssm.at[j], rsm.at[j], peer))
        for c in copies:
            c.start()
        for c in copies:
            c.wait_recv()
        pending.extend(copies)

    lane = lax.broadcasted_iota(jnp.int32, (NF, 128), 1)

    def center_body(q, carry):
        tw, tm = carry
        cols = pl.ds(pl.multiple_of(q * 2048, 2048), 2048)
        wv = w_ref[:, cols]
        return tw + wv, tm + ms_ref[:, cols] * wv

    tw, tm = lax.fori_loop(
        0, AL // 2048, center_body, (jnp.zeros((1, 2048), F32), jnp.zeros((3, 2048), F32))
    )
    tw = jnp.sum(tw, axis=1, keepdims=True)
    tm = jnp.sum(tm, axis=1, keepdims=True)
    lc = tm / tw

    def sums_body(q, acc):
        acc = list(acc)
        cols = pl.ds(pl.multiple_of(q * STEP, STEP), STEP)
        wv = w_ref[:, cols]
        wm = (ms_ref[:, cols] - lc) * wv
        for t in range(STEP // 128):
            lo = t * 128
            sub = pl.ds(pl.multiple_of(q * STEP + lo, 128), 128)
            wt = jnp.broadcast_to(wv[:, lo : lo + 128], (NF, 128))
            mt = [jnp.broadcast_to(wm[i : i + 1, lo : lo + 128], (NF, 128)) for i in range(3)]
            for j in range(3):
                xj = xv[j, :, sub]
                acc[j] = acc[j] + xj * wt
                for i in range(3):
                    acc[3 + i * 3 + j] = acc[3 + i * 3 + j] + xj * mt[i]
        return tuple(acc)

    acc = tuple(jnp.zeros((NF, 128), F32) for _ in range(12))
    per = CW // STEP
    for q in range(CHUNKS):
        loads[q].wait()
        acc = lax.fori_loop(q * per, (q + 1) * per, sums_body, acc)
    cols16 = [jnp.broadcast_to(tw, (NF, 1))] + [jnp.broadcast_to(tm[i : i + 1], (NF, 1)) for i in range(3)]
    cols16 += [jnp.sum(a, axis=1, keepdims=True) for a in acc]
    tile = jnp.zeros((NF, 128), F32)
    for q, col in enumerate(cols16):
        tile = jnp.where(lane == q, jnp.broadcast_to(col, (NF, 128)), tile)
    ex1[0] = tile
    pl.semaphore_wait(barrier, len(y_peers) + len(xc_peers) + len(z_peers))
    exchange(ex1, y_peers, y1s, y1r)

    slots = [ex1[j] for j in range(NY)]
    part = [[s[:, q : q + 1] for q in range(16)] for s in slots]
    total = part[0][0] + part[1][0] + part[2][0] + part[3][0]
    mc = [(part[0][1 + i] + part[1][1 + i] + part[2][1 + i] + part[3][1 + i]) / total for i in range(3)]
    fc = [(part[0][4 + j] + part[1][4 + j] + part[2][4 + j] + part[3][4 + j]) / total for j in range(3)]
    moment = []
    shift_c = [[p[1 + i] / p[0] - mc[i] for i in range(3)] for p in part]
    for i in range(3):
        for j in range(3):
            m = None
            for p, sc in zip(part, shift_c):
                term = p[7 + i * 3 + j] + sc[i] * p[4 + j]
                m = term if m is None else m + term
            moment.append(m / total)
    r = newton(moment)
    for q in range(9):
        rot[q] = jnp.broadcast_to(r[q], (NF, 128))
    for i in range(3):
        off = r[3 * i] * fc[0] + r[3 * i + 1] * fc[1] + r[3 * i + 2] * fc[2]
        rot[9 + i] = jnp.broadcast_to(mc[i] - off, (NF, 128))

    sload.wait()

    def move_body(own):
        def body(b, acc):
            core = pc if own else 1 - pc
            base = (b * NC + core) * BLK
            for i in range(3):
                pieces = []
                for t in range(BLK // 128):
                    sub = pl.ds(pl.multiple_of(base + t * 128, 128), 128)
                    v = rot[3 * i] * xv[0, :, sub] + rot[3 * i + 1] * xv[1, :, sub] + rot[3 * i + 2] * xv[2, :, sub]
                    v = v + rot[9 + i] - jnp.broadcast_to(ms_ref[i : i + 1, sub], (NF, 128))
                    pieces.append(v)
                v = jnp.concatenate(pieces, axis=1)
                v = jnp.concatenate([v, jnp.zeros((FP - NF, BLK), F32)], axis=0).astype(BF16)
                if own:
                    dall[b, i, 0:FP, :] = v
                else:
                    dsend[b, i] = v
                cols = pl.ds(pl.multiple_of(base, 128), BLK)
                acc = acc + lax.dot_general(sv[i, :, cols], v, NT, preferred_element_type=F32)
            return acc

        return body

    pacc = lax.fori_loop(0, NB, move_body(False), jnp.zeros((K, FP), F32))
    dcopy = remote(dsend, dall.at[:, :, FP : 2 * FP, :], dx_s, dx_r, partner)
    dcopy.start()
    pacc = lax.fori_loop(0, NB, move_body(True), pacc)

    ex2[0] = jnp.zeros((K, 128), F32)
    ex2[0, :, 0:FP] = pacc
    exchange(ex2, y_peers, y2s, y2r)
    ptot = ex2[0] + ex2[1] + ex2[2] + ex2[3]
    pp[0] = ptot
    pcopy = remote(pp.at[0], pp.at[1], pp_s, pp_r, partner)
    pcopy.start()
    rows = lax.broadcasted_iota(jnp.int32, (K, 128), 0)
    lanes = lax.broadcasted_iota(jnp.int32, (K, 128), 1)
    col = jnp.broadcast_to(jnp.sum(ptot, axis=1, keepdims=True), (K, 128))
    row = jnp.sum(jnp.where(rows == lanes, col, 0.0), axis=0, keepdims=True)
    pbx[0] = jnp.broadcast_to(row, (8, 128))
    exchange(pbx, xc_peers, px_s, px_r)
    v = pbx[0]
    for j in range(1, NX * NC):
        v = v + pbx[j]
    pbz[0] = v
    exchange(pbz, z_peers, pz_s, pz_r)
    v = pbz[0]
    for j in range(1, NZ):
        v = v + pbz[j]
    row = jnp.broadcast_to(v[0:1], (K, 128))
    pbar = jnp.sum(jnp.where(rows == lanes, row, 0.0), axis=1, keepdims=True) / FRAMES
    pcopy.wait_recv()
    other = pltpu.roll(pp[1], FP, 1)
    both = jnp.where(lanes < FP, ptot, other) - pbar
    cpt[...] = both.astype(BF16)
    dcopy.wait_recv()

    erow = lax.broadcasted_iota(jnp.int32, (16, 2 * FP), 0)
    ones = [jnp.where(erow == i, 1.0, 0.0).astype(BF16) for i in range(3)]

    def mm(lhs, rhs):
        return jnp.dot(lhs, rhs, preferred_element_type=F32)

    def term_a(dest, h, emit):
        def body(q, c):
            blk = dest * NZ + h * (NZ // 2) + q
            for i in range(2):
                emit(q, i, mm(cpt[:, 0 : 2 * FP], dall[blk, i]))
            return c

        lax.fori_loop(0, NZ // 2, body, 0)

    def term_b(dest, h, emit):
        def body(q, c):
            blk = (h * (NX // 2) + q) * NZ + dest
            emit(q, 0, mm(cpt[:, 0 : 2 * FP], dall[blk, 2]))
            sh = mm(ones[0], dall[blk, 0]) + mm(ones[1], dall[blk, 1]) + mm(ones[2], dall[blk, 2])
            emit(q, 1, sh)
            return c

        lax.fori_loop(0, NX // 2, body, 0)

    def rowslice(i):
        return slice(32 * i, 32 * i + 32)

    def brow(i):
        return slice(0, 32) if i == 0 else slice(32, 48)

    class Stage:
        def __init__(self, length, pos, sbuf, rbuf, ssm, rsm, fill, peer_of, cut):
            self.length, self.pos, self.sbuf, self.rbuf = length, pos, sbuf, rbuf
            self.ssm, self.rsm, self.fill, self.peer_of, self.cut = ssm, rsm, fill, peer_of, cut
            self.copies = {}

        def send(self, st, s):
            h, d = STREAMS[st]
            total_steps = steps_of(self.length, h, d)
            if s >= total_steps:
                return
            dest = (self.pos + (d * (total_steps - s) + self.length)) % self.length
            if s == 0:
                src = self.sbuf.at[st]
                self.fill(src, dest, h, False)
            else:
                self.copies[st, s - 1].wait_recv()
                src = self.rbuf.at[st, s - 1]
                self.fill(src, dest, h, True)
            c = remote(
                self.cut(src, h), self.cut(self.rbuf.at[st, s], h), self.ssm.at[st, s], self.rsm.at[st, s],
                self.peer_of(d),
            )
            c.start()
            pending.append(c)
            self.copies[st, s] = c

        def finals(self, h):
            out = []
            for st, (hh, d) in enumerate(STREAMS):
                if hh == h:
                    s = steps_of(self.length, h, d) - 1
                    self.copies[st, s].wait_recv()
                    out.append(self.rbuf.at[st, s])
            return out

    def fill_a1(ref, dest, h, add):
        def emit(q, i, t):
            if add:
                t = t + ref[q, rowslice(i), :].astype(F32)
            ref[q, rowslice(i), :] = t.astype(BF16)

        term_a(dest, h, emit)

    def fill_b1(ref, dest, h, add):
        def emit(q, i, t):
            if add:
                t = t + ref[q, brow(i), :].astype(F32)
            ref[q, brow(i), :] = t.astype(BF16)

        term_b(dest, h, emit)

    def fill_a2(ref, dest, h, add):
        t = acca[dest, rowslice(h), :]
        if add:
            t = t + ref[...].astype(F32)
        ref[...] = t.astype(BF16)

    def fill_b2(ref, dest, h, add):
        if h == 0:
            t = accb[dest, 0:32, :]
            if add:
                t = t + ref[...].astype(F32)
            ref[...] = t.astype(BF16)
        else:
            t = accb[dest, 32:48, :]
            if add:
                t = t + ref[0:16, :].astype(F32)
            ref[0:16, :] = t.astype(BF16)

    def whole(ref, h):
        return ref

    def cut_b2(ref, h):
        return ref if h == 0 else ref.at[0:16, :]

    x_dir = {1: dev(dx=1), -1: dev(dx=-1)}
    z_dir = {1: dev(dz=1), -1: dev(dz=-1)}
    sa1 = Stage(NX, px, a1s, a1r, a1ss, a1rs, fill_a1, x_dir.get, whole)
    sb1 = Stage(NZ, pz, b1s, b1r, b1ss, b1rs, fill_b1, z_dir.get, whole)
    sa2 = Stage(NZ, pz, a2s, a2r, a2ss, a2rs, fill_a2, z_dir.get, whole)
    sb2 = Stage(NX, px, b2s, b2r, b2ss, b2rs, fill_b2, x_dir.get, cut_b2)

    order = (0, 3, 2, 1)
    for st in order:
        sa1.send(st, 0)
        sb1.send(st, 0)
    for st in order:
        sb1.send(st, 1)
    for st in order:
        sa1.send(st, 1)
    for st in order:
        sb1.send(st, 2)
    for st in order:
        sb1.send(st, 3)

    for h in (0, 1):
        f0, f1 = sa1.finals(h)

        def emit(q, i, t, f0=f0, f1=f1, h=h):
            t = t + f0[q, rowslice(i), :].astype(F32) + f1[q, rowslice(i), :].astype(F32)
            acca[h * (NZ // 2) + q, rowslice(i), :] = t

        term_a(px, h, emit)
    for st in order:
        sa2.send(st, 0)
    for h in (0, 1):
        f0, f1 = sb1.finals(h)

        def emit(q, i, t, f0=f0, f1=f1, h=h):
            t = t + f0[q, brow(i), :].astype(F32) + f1[q, brow(i), :].astype(F32)
            accb[h * (NX // 2) + q, brow(i), :] = t

        term_b(pz, h, emit)
    for st in order:
        sb2.send(st, 0)
    for st in order:
        sa2.send(st, 1)
    for st in order:
        sb2.send(st, 1)
    for st in order:
        sa2.send(st, 2)
    for st in order:
        sa2.send(st, 3)

    inv_f = 1.0 / FRAMES
    f0, f1 = sb2.finals(0)
    img2 = (accb[px, 0:32, :] + f0[...].astype(F32) + f1[...].astype(F32)) * inv_f
    f0, f1 = sb2.finals(1)
    shift = accb[px, 32:48, :] + f0[0:16, :].astype(F32) + f1[0:16, :].astype(F32)
    own = pl.ds(pl.multiple_of(n * BLK, 128), BLK)
    nm_ref[...] = ms_ref[:, own] + shift[0:3] * inv_f
    imgs = []
    for h in (0, 1):
        f0, f1 = sa2.finals(h)
        imgs.append((acca[pz, rowslice(h), :] + f0[...].astype(F32) + f1[...].astype(F32)) * inv_f)
    imgs.append(img2)
    g = None
    for i in range(3):
        img_ref[i] = imgs[i]
        t = lax.dot_general(imgs[i], imgs[i], NT, preferred_element_type=F32, precision=HIGHEST)
        g = t if g is None else g + t
    gsq[...] = jnp.zeros((K, 128), F32)
    gsq[:, 0:K] = g
    v = gsq[0:8, :]
    for q in range(1, 4):
        v = v + pltpu.roll(gsq[8 * q : 8 * q + 8, :], 32 * q, 1)
    gx[0] = v
    exchange(gx, xc_peers, gx_s, gx_r)
    v = gx[0]
    for j in range(1, NX * NC):
        v = v + gx[j]
    gy[0] = v
    exchange(gy, y_peers, gy_s, gy_r)
    gz[0] = gy[0] + gy[1] + gy[2] + gy[3]
    exchange(gz, z_peers, gz_s, gz_r)
    v = gz[0]
    for j in range(1, NZ):
        v = v + gz[j]
    v = v / (3 * ATOMS)
    m = jnp.concatenate([v] + [pltpu.roll(v, 128 - 32 * q, 1) for q in range(1, 4)], axis=0)
    m = jnp.where(lanes < K, m, jnp.where(lanes - K == rows, 1.0, 0.0))
    for j in range(K - 1):
        prow = jnp.broadcast_to(m[j : j + 1, :], (K, 128))
        pcol = jnp.broadcast_to(m[:, j : j + 1], (K, 128))
        piv = 1.0 / pcol[j : j + 1, :]
        m = jnp.where(rows > j, m - pcol * (prow * piv), m)
    diag = jnp.sum(jnp.where(rows == lanes, m, 0.0), axis=1, keepdims=True)
    linv = pltpu.roll(m, 128 - K, 1) * (1.0 / jnp.sqrt(diag))
    linv = linv[:, 0:K]
    for i in range(3):
        bas_ref[i] = jnp.dot(linv, imgs[i], preferred_element_type=F32, precision=HIGHEST)

    for c in pending + [dcopy, pcopy]:
        c.wait_send()


def per_device(frames, mean_structure, atom_weight, subspace):
    x = jnp.transpose(frames, (1, 0, 2))
    s = jnp.transpose(subspace, (1, 0, 2))
    vm = pl.BlockSpec(memory_space=pltpu.VMEM)
    anyspec = pl.BlockSpec(memory_space=pl.ANY)
    dma = pltpu.SemaphoreType.DMA
    V = pltpu.VMEM
    scratch = [
        V((3, NF, AL), F32), V((3, K, AL), BF16), V((NB, 3, 2 * FP, BLK), BF16), V((NB, 3, FP, BLK), BF16),
        V((12, NF, 128), F32), V((NY, NF, 128), F32), V((NY, K, 128), F32), V((2, K, 128), F32), V((K, 128), F32),
        V((NX * NC, 8, 128), F32), V((NZ, 8, 128), F32), V((K, 128), BF16),
        V((NX * NC, 8, 128), F32), V((NY, 8, 128), F32), V((NZ, 8, 128), F32),
        V((4, NZ // 2, 64, BLK), BF16), V((4, NX // 2, NZ // 2, 64, BLK), BF16),
        V((4, NX // 2, 48, BLK), BF16), V((4, NZ // 2, NX // 2, 48, BLK), BF16),
        V((4, 32, BLK), BF16), V((4, NZ // 2, 32, BLK), BF16),
        V((4, 32, BLK), BF16), V((4, NX // 2, 32, BLK), BF16),
        V((NZ, 64, BLK), F32), V((NX, 48, BLK), F32),
        dma((CHUNKS,)), dma,
        dma((NY - 1,)), dma((NY - 1,)), dma((NY - 1,)), dma((NY - 1,)),
        dma((NX * NC - 1,)), dma((NX * NC - 1,)), dma((NZ - 1,)), dma((NZ - 1,)),
        dma, dma, dma, dma,
        dma((NX * NC - 1,)), dma((NX * NC - 1,)), dma((NY - 1,)), dma((NY - 1,)), dma((NZ - 1,)), dma((NZ - 1,)),
        dma((4, NX // 2)), dma((4, NX // 2)), dma((4, NZ // 2)), dma((4, NZ // 2)),
        dma((4, NZ // 2)), dma((4, NZ // 2)), dma((4, NX // 2)), dma((4, NX // 2)),
    ]
    nm, img, bas = pl.pallas_call(
        kernel,
        out_shape=(
            jax.ShapeDtypeStruct((3, BLK), F32),
            jax.ShapeDtypeStruct((3, K, BLK), F32),
            jax.ShapeDtypeStruct((3, K, BLK), F32),
        ),
        in_specs=[anyspec, vm, vm, anyspec],
        out_specs=(vm, vm, vm),
        scratch_shapes=scratch,
        compiler_params=pltpu.CompilerParams(
            collective_id=0, has_side_effects=True, vmem_limit_bytes=60 * 1024 * 1024
        ),
    )(x, mean_structure, atom_weight.reshape(1, AL), s)
    return nm, jnp.transpose(img, (1, 0, 2)), jnp.transpose(bas, (1, 0, 2))


def solution(mesh):
    return jax.shard_map(
        per_device,
        mesh=mesh,
        in_specs=(P("frames", None, "atoms"), P(None, "atoms"), P("atoms"), P(None, None, "atoms")),
        out_specs=(
            P(None, ("atoms", "frames")),
            P(None, None, ("atoms", "frames")),
            P(None, None, ("atoms", "frames")),
        ),
        check_vma=False,
    )
```

time: 464 us -> 93.6 us (0.20)
  blocking collectives: 200 us -> 0 us
  waiting for transfers between devices: 144 us -> 0 us
  Pallas kernels: 0 us -> 88.3 us
  matrix products: 76.6 us -> 0 us
  other arithmetic: 21.2 us -> 0 us
  between operations: 14.9 us -> 0.64 us
    psum x5 -> x0, blocking collectives: 200 us -> none  [the longest x1 87.8 us: per_device(): proj_total = lax.psum(jnp.sum(local_proj, axis=0), ('atoms', 'frames'))]
    reduce_scatter x1 -> x0, waiting for transfers between devices: 144 us -> none  [per_device(): lax.psum_scatter(stacked, 'frames', scatter_dimension=2, tiled=True)]
    pallas_call x0 -> x1, Pallas kernels: none -> 88.3 us  [per_device(): pl.pallas_call(kernel, out_shape=(jax.ShapeDtypeStruct((3, BLK), F32), ja...]
    dot_general x7 -> x0, matrix products: 74.7 us -> none  [the longest x1 29.3 us: per_device(): moved = jnp.einsum('fij,fja->fia', rotation, frames, precision=highest)]
    another operation x29 -> x0, other arithmetic: 7.57 us -> none  [the longest x3 3.59 us: per_device(): lower = jnp.linalg.cholesky(gram)]
    concatenate x1 -> x0, other arithmetic: 5.66 us -> none  [per_device(): stacked = jnp.concatenate([term, shift_sum[None]], axis=0)]
  transfers between devices with their start and end apart: 1 -> 0, of which waited for: 1 -> 0; matrix products, arithmetic and copies ran while one was open for 0% -> 0% of each run, Pallas kernels for 0% -> 0%
where the time goes in v1:
time: 93.6 us; the launch traced here: 93.4 us
  Pallas kernels  88.3 us (94%)
  local copies, waits for them, and re-layouts  4.45 us (5%)
    pallas_call x1, Pallas kernels, per_device(): pl.pallas_call(kernel, out_shape=(jax.ShapeDtypeStruct((3, BLK), F32), ja...  88.3 us
    unnamed x3, local copies, waits for them, and re-layouts  4.45 us

profile of v1, /device:TPU:1, one launch (start us, length us, event | category | flops | bytes accessed | tf_op | source)
XLA Modules:
  0.0 93.4 jit_solution(12565095287073349278)
XLA Ops:
  0.6 88.3 %shard_map.67 = (f32[3,384]{1,0:T(4,128)}, f32[3,32,384]{2,1,0:T(8,128)}, f32[3,32,384]{2,1,0:T(8,128)}) custom-call(f32[3,24,24576]{2,1,0:T(8,128)} %bitcast.5, f32[3,24576]{1,0:T(4,128)} %ms_ref.1, f32[1,24576]{1,0:T(1,128)} %bitcast.9, bf16[3,32,24576]{2,1,0:T(8,128)(2,1)} %bitcast.6), custom_call_target="tpu_custom_call" | custom-call | tf_op jit(solution)/shard_map/pallas_call | solution.py:471
  88.9 1.3 %copy.10 = f32[3,384]{1,0:T(4,128)} copy(f32[3,384]{1,0:T(4,128)} %get-tuple-element.12) | data formatting | bytes 9216
  90.2 1.6 %copy.11 = f32[32,3,384]{2,0,1:T(8,128)} copy(f32[32,3,384]{2,0,1:T(8,128)} %bitcast.8) | data formatting | bytes 294912
  91.8 1.6 %copy.12 = f32[32,3,384]{2,0,1:T(8,128)} copy(f32[32,3,384]{2,0,1:T(8,128)} %bitcast.7) | data formatting | bytes 294912

commit v2 on v1

--- a/solution.py
+++ b/solution.py
@@ -18,6 +18,8 @@
 CHUNKS = 8
 CW = AL // CHUNKS
 STEP = 512
+UNROLL = 8
+VLHS = False
 F32 = jnp.float32
 BF16 = jnp.bfloat16
 MESH = pl.DeviceIdType.MESH
@@ -56,11 +58,11 @@
 
 
 def kernel(
-    x_hbm, ms_ref, w_ref, s_hbm, nm_ref, img_ref, bas_ref,
-    xv, sv, dall, dsend, rot, ex1, ex2, pp, gsq, pbx, pbz, cpt, gx, gy, gz,
+    x_hbm, ms_ref, w_ref, s_hbm, nm_ref, img_ref, g_ref,
+    xv, sv, dall, dsend, rot, ex1, ex2, pp, gsq, pba, cpt, gx, gz,
     a1s, a1r, b1s, b1r, a2s, a2r, b2s, b2r, acca, accb,
-    xsem, ssem, y1s, y1r, y2s, y2r, px_s, px_r, pz_s, pz_r, pp_s, pp_r, dx_s, dx_r,
-    gx_s, gx_r, gy_s, gy_r, gz_s, gz_r, a1ss, a1rs, b1ss, b1rs, a2ss, a2rs, b2ss, b2rs,
+    xsem, ssem, y1s, y1r, y2s, y2r, px_s, px_r, pp_s, pp_r, dx_s, dx_r,
+    gx_s, gx_r, gz_s, gz_r, a1ss, a1rs, b1ss, b1rs, a2ss, a2rs, b2ss, b2rs,
 ):
     y = lax.axis_index("atoms")
     n = lax.axis_index("frames")
@@ -75,7 +77,9 @@
         return ((y + dy) % NY, (tx * NZ + tz) * NC + tc)
 
     y_peers = [dev(dy=j) for j in range(1, NY)]
-    xc_peers = [dev(dx=j // 2, dc=j % 2) for j in range(1, NX * NC)]
+    f_peers = [dev(dx=j // (NZ * NC), dz=(j // NC) % NZ, dc=j % NC) for j in range(1, NB * NC)]
+    p_peers = [dev(dy=j // (NX * NC), dx=(j // NC) % NX, dc=j % NC) for j in range(1, NX * NC * NY)]
+    greet = f_peers + [p_peers[j - 1] for j in range(NX * NC, NX * NC * NY)]
     z_peers = [dev(dz=j) for j in range(1, NZ)]
     partner = dev(dc=1)
 
@@ -89,7 +93,7 @@
     sload.start()
 
     barrier = pltpu.get_barrier_semaphore()
-    for peer in y_peers + xc_peers + z_peers:
+    for peer in greet:
         pl.semaphore_signal(barrier, inc=1, device_id=peer, device_id_type=MESH)
 
     def remote(src, dst, ssm, rsm, peer):
@@ -146,65 +150,80 @@
     for q in range(CHUNKS):
         loads[q].wait()
         acc = lax.fori_loop(q * per, (q + 1) * per, sums_body, acc)
-    cols16 = [jnp.broadcast_to(tw, (NF, 1))] + [jnp.broadcast_to(tm[i : i + 1], (NF, 1)) for i in range(3)]
-    cols16 += [jnp.sum(a, axis=1, keepdims=True) for a in acc]
-    tile = jnp.zeros((NF, 128), F32)
-    for q, col in enumerate(cols16):
-        tile = jnp.where(lane == q, jnp.broadcast_to(col, (NF, 128)), tile)
-    ex1[0] = tile
-    pl.semaphore_wait(barrier, len(y_peers) + len(xc_peers) + len(z_peers))
-    exchange(ex1, y_peers, y1s, y1r)
-
-    slots = [ex1[j] for j in range(NY)]
-    part = [[s[:, q : q + 1] for q in range(16)] for s in slots]
-    total = part[0][0] + part[1][0] + part[2][0] + part[3][0]
-    mc = [(part[0][1 + i] + part[1][1 + i] + part[2][1 + i] + part[3][1 + i]) / total for i in range(3)]
-    fc = [(part[0][4 + j] + part[1][4 + j] + part[2][4 + j] + part[3][4 + j]) / total for j in range(3)]
-    moment = []
-    shift_c = [[p[1 + i] / p[0] - mc[i] for i in range(3)] for p in part]
+    sums = [jnp.broadcast_to(jnp.sum(a, axis=1, keepdims=True), (NF, 128)) for a in acc]
+    wide = [jnp.broadcast_to(lc[i : i + 1], (NF, 128)) for i in range(3)]
+    wide_m = [jnp.broadcast_to(tm[i : i + 1], (NF, 128)) for i in range(3)]
+    tile = jnp.broadcast_to(tw, (NF, 128))
     for i in range(3):
         for j in range(3):
-            m = None
-            for p, sc in zip(part, shift_c):
-                term = p[7 + i * 3 + j] + sc[i] * p[4 + j]
-                m = term if m is None else m + term
-            moment.append(m / total)
-    r = newton(moment)
+            e = 3 * i + j
+            tile = jnp.where(lane == e, sums[3 + e], tile)
+            tile = jnp.where(lane == 16 + e, sums[j], tile)
+            tile = jnp.where(lane == 32 + e, wide[i], tile)
+            tile = jnp.where(lane == 48 + e, wide_m[i], tile)
+    ex1[0] = tile
+    pl.semaphore_wait(barrier, len(greet))
+    exchange(ex1, y_peers, y1s, y1r)
+
+    slots = [ex1[j] for j in range(NY)]
+    tsum = slots[0] + slots[1] + slots[2] + slots[3]
+    inv_total = 1.0 / jnp.broadcast_to(tsum[:, 127:128], (NF, 128))
+    tsum = tsum * inv_total
+    mrep = pltpu.roll(tsum, 128 - 48, 1)
+    packed = None
+    for p in slots:
+        t = p + (pltpu.roll(p, 128 - 32, 1) - mrep) * pltpu.roll(p, 128 - 16, 1)
+        packed = t if packed is None else packed + t
+    packed = packed * inv_total
+    r = newton([jnp.broadcast_to(packed[:, q : q + 1], (NF, 128)) for q in range(9)])
+    fc = [jnp.broadcast_to(tsum[:, 16 + j : 17 + j], (NF, 128)) for j in range(3)]
+    mc = [jnp.broadcast_to(tsum[:, 48 + 3 * i : 49 + 3 * i], (NF, 128)) for i in range(3)]
     for q in range(9):
-        rot[q] = jnp.broadcast_to(r[q], (NF, 128))
+        rot[q] = r[q]
     for i in range(3):
         off = r[3 * i] * fc[0] + r[3 * i + 1] * fc[1] + r[3 * i + 2] * fc[2]
-        rot[9 + i] = jnp.broadcast_to(mc[i] - off, (NF, 128))
+        rot[9 + i] = mc[i] - off
 
     sload.wait()
 
     def move_body(own):
-        def body(b, acc):
+        def body(g, acc):
             core = pc if own else 1 - pc
-            base = (b * NC + core) * BLK
             for i in range(3):
-                pieces = []
-                for t in range(BLK // 128):
-                    sub = pl.ds(pl.multiple_of(base + t * 128, 128), 128)
-                    v = rot[3 * i] * xv[0, :, sub] + rot[3 * i + 1] * xv[1, :, sub] + rot[3 * i + 2] * xv[2, :, sub]
-                    v = v + rot[9 + i] - jnp.broadcast_to(ms_ref[i : i + 1, sub], (NF, 128))
-                    pieces.append(v)
-                v = jnp.concatenate(pieces, axis=1)
-                v = jnp.concatenate([v, jnp.zeros((FP - NF, BLK), F32)], axis=0).astype(BF16)
-                if own:
-                    dall[b, i, 0:FP, :] = v
+                vs, ss = [], []
+                for u in range(UNROLL):
+                    b = g * UNROLL + u
+                    base = (b * NC + core) * BLK
+                    pieces = []
+                    for t in range(BLK // 128):
+                        sub = pl.ds(pl.multiple_of(base + t * 128, 128), 128)
+                        v = rot[3 * i] * xv[0, :, sub] + rot[3 * i + 1] * xv[1, :, sub] + rot[3 * i + 2] * xv[2, :, sub]
+                        v = v + rot[9 + i] - jnp.broadcast_to(ms_ref[i : i + 1, sub], (NF, 128))
+                        pieces.append(v)
+                    v = jnp.concatenate(pieces, axis=1)
+                    v = jnp.concatenate([v, jnp.zeros((FP - NF, BLK), F32)], axis=0).astype(BF16)
+                    if own:
+                        dall[b, i, 0:FP, :] = v
+                    else:
+                        dsend[b, i] = v
+                    vs.append(v)
+                    ss.append(sv[i, :, pl.ds(pl.multiple_of(base, 128), BLK)])
+                vs = jnp.concatenate(vs, axis=1)
+                ss = jnp.concatenate(ss, axis=1)
+                if VLHS:
+                    acc = acc + lax.dot_general(vs, ss, NT, preferred_element_type=F32)
                 else:
-                    dsend[b, i] = v
-                cols = pl.ds(pl.multiple_of(base, 128), BLK)
-                acc = acc + lax.dot_general(sv[i, :, cols], v, NT, preferred_element_type=F32)
+                    acc = acc + lax.dot_general(ss, vs, NT, preferred_element_type=F32)
             return acc
 
         return body
 
-    pacc = lax.fori_loop(0, NB, move_body(False), jnp.zeros((K, FP), F32))
+    pacc = lax.fori_loop(0, NB // UNROLL, move_body(False), jnp.zeros((K, FP), F32))
     dcopy = remote(dsend, dall.at[:, :, FP : 2 * FP, :], dx_s, dx_r, partner)
     dcopy.start()
-    pacc = lax.fori_loop(0, NB, move_body(True), pacc)
+    pacc = lax.fori_loop(0, NB // UNROLL, move_body(True), pacc)
+    if VLHS:
+        pacc = pacc.T
 
     ex2[0] = jnp.zeros((K, 128), F32)
     ex2[0, :, 0:FP] = pacc
@@ -217,17 +236,9 @@
     lanes = lax.broadcasted_iota(jnp.int32, (K, 128), 1)
     col = jnp.broadcast_to(jnp.sum(ptot, axis=1, keepdims=True), (K, 128))
     row = jnp.sum(jnp.where(rows == lanes, col, 0.0), axis=0, keepdims=True)
-    pbx[0] = jnp.broadcast_to(row, (8, 128))
-    exchange(pbx, xc_peers, px_s, px_r)
-    v = pbx[0]
-    for j in range(1, NX * NC):
-        v = v + pbx[j]
-    pbz[0] = v
-    exchange(pbz, z_peers, pz_s, pz_r)
-    v = pbz[0]
-    for j in range(1, NZ):
-        v = v + pbz[j]
-    row = jnp.broadcast_to(v[0:1], (K, 128))
+    pba[0] = row
+    exchange(pba, f_peers, px_s, px_r)
+    row = jnp.broadcast_to(jnp.sum(pba[...], axis=0), (K, 128))
     pbar = jnp.sum(jnp.where(rows == lanes, row, 0.0), axis=1, keepdims=True) / FRAMES
     pcopy.wait_recv()
     other = pltpu.roll(pp[1], FP, 1)
@@ -414,18 +425,22 @@
     for q in range(1, 4):
         v = v + pltpu.roll(gsq[8 * q : 8 * q + 8, :], 32 * q, 1)
     gx[0] = v
-    exchange(gx, xc_peers, gx_s, gx_r)
-    v = gx[0]
-    for j in range(1, NX * NC):
-        v = v + gx[j]
-    gy[0] = v
-    exchange(gy, y_peers, gy_s, gy_r)
-    gz[0] = gy[0] + gy[1] + gy[2] + gy[3]
+    exchange(gx, p_peers, gx_s, gx_r)
+    gz[0] = jnp.sum(gx[...], axis=0)
     exchange(gz, z_peers, gz_s, gz_r)
     v = gz[0]
     for j in range(1, NZ):
         v = v + gz[j]
-    v = v / (3 * ATOMS)
+    g_ref[...] = v / (3 * ATOMS)
+
+    for c in pending + [dcopy, pcopy]:
+        c.wait_send()
+
+
+def finish(nm_in, img_in, g_ref, nm_ref, img_ref, bas_ref):
+    rows = lax.broadcasted_iota(jnp.int32, (K, 128), 0)
+    lanes = lax.broadcasted_iota(jnp.int32, (K, 128), 1)
+    v = g_ref[...]
     m = jnp.concatenate([v] + [pltpu.roll(v, 128 - 32 * q, 1) for q in range(1, 4)], axis=0)
     m = jnp.where(lanes < K, m, jnp.where(lanes - K == rows, 1.0, 0.0))
     for j in range(K - 1):
@@ -437,10 +452,9 @@
     linv = pltpu.roll(m, 128 - K, 1) * (1.0 / jnp.sqrt(diag))
     linv = linv[:, 0:K]
     for i in range(3):
-        bas_ref[i] = jnp.dot(linv, imgs[i], preferred_element_type=F32, precision=HIGHEST)
-
-    for c in pending + [dcopy, pcopy]:
-        c.wait_send()
+        bas_ref[i] = jnp.dot(linv, img_in[i], preferred_element_type=F32, precision=HIGHEST)
+        img_ref[i] = img_in[i]
+    nm_ref[...] = nm_in[...]
 
 
 def per_device(frames, mean_structure, atom_weight, subspace):
@@ -453,8 +467,8 @@
     scratch = [
         V((3, NF, AL), F32), V((3, K, AL), BF16), V((NB, 3, 2 * FP, BLK), BF16), V((NB, 3, FP, BLK), BF16),
         V((12, NF, 128), F32), V((NY, NF, 128), F32), V((NY, K, 128), F32), V((2, K, 128), F32), V((K, 128), F32),
-        V((NX * NC, 8, 128), F32), V((NZ, 8, 128), F32), V((K, 128), BF16),
-        V((NX * NC, 8, 128), F32), V((NY, 8, 128), F32), V((NZ, 8, 128), F32),
+        V((NB * NC, 1, 128), F32), V((K, 128), BF16),
+        V((NX * NC * NY, 8, 128), F32), V((NZ, 8, 128), F32),
         V((4, NZ // 2, 64, BLK), BF16), V((4, NX // 2, NZ // 2, 64, BLK), BF16),
         V((4, NX // 2, 48, BLK), BF16), V((4, NZ // 2, NX // 2, 48, BLK), BF16),
         V((4, 32, BLK), BF16), V((4, NZ // 2, 32, BLK), BF16),
@@ -462,19 +476,16 @@
         V((NZ, 64, BLK), F32), V((NX, 48, BLK), F32),
         dma((CHUNKS,)), dma,
         dma((NY - 1,)), dma((NY - 1,)), dma((NY - 1,)), dma((NY - 1,)),
-        dma((NX * NC - 1,)), dma((NX * NC - 1,)), dma((NZ - 1,)), dma((NZ - 1,)),
+        dma((NB * NC - 1,)), dma((NB * NC - 1,)),
         dma, dma, dma, dma,
-        dma((NX * NC - 1,)), dma((NX * NC - 1,)), dma((NY - 1,)), dma((NY - 1,)), dma((NZ - 1,)), dma((NZ - 1,)),
+        dma((NX * NC * NY - 1,)), dma((NX * NC * NY - 1,)), dma((NZ - 1,)), dma((NZ - 1,)),
         dma((4, NX // 2)), dma((4, NX // 2)), dma((4, NZ // 2)), dma((4, NZ // 2)),
         dma((4, NZ // 2)), dma((4, NZ // 2)), dma((4, NX // 2)), dma((4, NX // 2)),
     ]
-    nm, img, bas = pl.pallas_call(
+    shapes = [(3, BLK), (3, K, BLK), (8, 128)]
+    nm, img, gram = pl.pallas_call(
         kernel,
-        out_shape=(
-            jax.ShapeDtypeStruct((3, BLK), F32),
-            jax.ShapeDtypeStruct((3, K, BLK), F32),
-            jax.ShapeDtypeStruct((3, K, BLK), F32),
-        ),
+        out_shape=tuple(jax.ShapeDtypeStruct(d, F32) for d in shapes),
         in_specs=[anyspec, vm, vm, anyspec],
         out_specs=(vm, vm, vm),
         scratch_shapes=scratch,
@@ -482,6 +493,13 @@
             collective_id=0, has_side_effects=True, vmem_limit_bytes=60 * 1024 * 1024
         ),
     )(x, mean_structure, atom_weight.reshape(1, AL), s)
+    shapes = [(3, BLK), (3, K, BLK), (3, K, BLK)]
+    nm, img, bas = pl.pallas_call(
+        finish,
+        out_shape=tuple(jax.ShapeDtypeStruct(d, F32) for d in shapes),
+        in_specs=[vm, vm, vm],
+        out_specs=(vm, vm, vm),
+    )(nm, img, gram)
     return nm, jnp.transpose(img, (1, 0, 2)), jnp.transpose(bas, (1, 0, 2))
 
 

time: 93.6 us -> 79.9 us (0.85)
  Pallas kernels: 88.3 us -> 79.2 us
  local copies, waits for them, and re-layouts: 4.45 us -> 0 us
    pallas_call x1 -> x2, Pallas kernels: 88.3 us -> 79.2 us  [the longest x1 74.7 us: per_device(): pl.pallas_call(kernel, out_shape=tuple((jax.ShapeDtypeStruct(d, F32) for...]
    unnamed x3 -> x0, local copies, waits for them, and re-layouts: 4.45 us -> none
where the time goes in v2:
time: 79.9 us; the launch traced here: 79.8 us
  Pallas kernels  79.2 us (99%)
    pallas_call x1, Pallas kernels, per_device(): pl.pallas_call(kernel, out_shape=tuple((jax.ShapeDtypeStruct(d, F32) for...  74.7 us
    pallas_call x1, Pallas kernels, per_device(): pl.pallas_call(finish, out_shape=tuple((jax.ShapeDtypeStruct(d, F32) for...  4.47 us

profile of v2, /device:TPU:1, one launch (start us, length us, event | category | flops | bytes accessed | tf_op | source)
XLA Modules:
  0.0 79.8 jit_solution(10062564386542699976)
XLA Ops:
  0.6 74.7 %shard_map.67 = (f32[3,384]{1,0:T(4,128)}, f32[3,32,384]{2,1,0:T(8,128)}, f32[8,128]{1,0:T(8,128)}) custom-call(f32[3,24,24576]{2,1,0:T(8,128)} %bitcast.5, f32[3,24576]{1,0:T(4,128)} %ms_ref.1, f32[1,24576]{1,0:T(1,128)} %bitcast.7, bf16[3,32,24576]{2,1,0:T(8,128)(2,1)} %bitcast.6), custom_call_target="tpu_custom_call" | custom-call | tf_op jit(solution)/shard_map/pallas_call | solution.py:486
  75.3 4.5 %shard_map.68 = (f32[3,384]{1,0:T(4,128)}, f32[3,32,384]{2,1,0:T(8,128)}, f32[3,32,384]{2,1,0:T(8,128)}) custom-call(f32[3,384]{1,0:T(4,128)} %get-tuple-element.9.nm_in, f32[3,32,384]{2,1,0:T(8,128)} %get-tuple-element.10.img_in, f32[8,128]{1,0:T(8,128)} %get-tuple-element.11.g_ref), custom_call_target="tpu_custom_call" | custom-call | tf_op jit(solution)/shard_map/pallas_call | solution.py:497

commit v3 on v2

--- a/solution.py
+++ b/solution.py
@@ -24,7 +24,7 @@
 BF16 = jnp.bfloat16
 MESH = pl.DeviceIdType.MESH
 HIGHEST = lax.Precision.HIGHEST
-STREAMS = tuple((h, d) for h in (0, 1) for d in (1, -1))
+PARTS = ((3, 4), (5, 2), (6, 1), (7, 0))
 NT = (((1,), (1,)), ((), ()))
 
 
@@ -58,10 +58,10 @@
 
 
 def kernel(
-    x_hbm, ms_ref, w_ref, s_hbm, nm_ref, img_ref, g_ref,
-    xv, sv, dall, dsend, rot, ex1, ex2, pp, gsq, pba, cpt, gx, gz,
-    a1s, a1r, b1s, b1r, a2s, a2r, b2s, b2r, acca, accb,
-    xsem, ssem, y1s, y1r, y2s, y2r, px_s, px_r, pp_s, pp_r, dx_s, dx_r,
+    x_hbm, ms_hbm, w_hbm, s_hbm, nm_ref, img_ref, g_ref,
+    ms_ref, w_ref, xv, sv, dall, dsend, rot, ex1, ex2, pp, gsq, pba, cpt, gx, gz,
+    a1s, a1r, b1s, b1r, a2s, a2r, b2s, b2r, acca, accb, taf, tbf,
+    msem, wsem, xsem, ssem, y1s, y1r, y2s, y2r, px_s, px_r, pp_s, pp_r, dx_s, dx_r,
     gx_s, gx_r, gz_s, gz_r, a1ss, a1rs, b1ss, b1rs, a2ss, a2rs, b2ss, b2rs,
 ):
     y = lax.axis_index("atoms")
@@ -83,14 +83,18 @@
     z_peers = [dev(dz=j) for j in range(1, NZ)]
     partner = dev(dc=1)
 
+    mload = pltpu.make_async_copy(ms_hbm, ms_ref, msem)
+    wload = pltpu.make_async_copy(w_hbm, w_ref, wsem)
+    wload.start()
+    mload.start()
     loads = []
     for q in range(CHUNKS):
         cols = pl.ds(q * CW, CW)
         cp = pltpu.make_async_copy(x_hbm.at[:, :, cols], xv.at[:, :, cols], xsem.at[q])
+        loads.append(cp)
+    for cp in loads[:2]:
         cp.start()
-        loads.append(cp)
     sload = pltpu.make_async_copy(s_hbm, sv, ssem)
-    sload.start()
 
     barrier = pltpu.get_barrier_semaphore()
     for peer in greet:
@@ -115,24 +119,19 @@
 
     lane = lax.broadcasted_iota(jnp.int32, (NF, 128), 1)
 
-    def center_body(q, carry):
-        tw, tm = carry
-        cols = pl.ds(pl.multiple_of(q * 2048, 2048), 2048)
-        wv = w_ref[:, cols]
-        return tw + wv, tm + ms_ref[:, cols] * wv
-
-    tw, tm = lax.fori_loop(
-        0, AL // 2048, center_body, (jnp.zeros((1, 2048), F32), jnp.zeros((3, 2048), F32))
-    )
-    tw = jnp.sum(tw, axis=1, keepdims=True)
-    tm = jnp.sum(tm, axis=1, keepdims=True)
-    lc = tm / tw
+    wload.wait()
+    mload.wait()
+    for cp in loads[2:]:
+        cp.start()
+    lc = jnp.sum(ms_ref[:, 0:2048], axis=1, keepdims=True) * (1.0 / 2048)
 
     def sums_body(q, acc):
         acc = list(acc)
+        tw, tm = acc[12:]
         cols = pl.ds(pl.multiple_of(q * STEP, STEP), STEP)
         wv = w_ref[:, cols]
         wm = (ms_ref[:, cols] - lc) * wv
+        acc[12:] = [tw + wv, tm + wm]
         for t in range(STEP // 128):
             lo = t * 128
             sub = pl.ds(pl.multiple_of(q * STEP + lo, 128), 128)
@@ -146,11 +145,16 @@
         return tuple(acc)
 
     acc = tuple(jnp.zeros((NF, 128), F32) for _ in range(12))
+    acc += (jnp.zeros((1, STEP), F32), jnp.zeros((3, STEP), F32))
     per = CW // STEP
     for q in range(CHUNKS):
+        if q == CHUNKS - 1:
+            sload.start()
         loads[q].wait()
         acc = lax.fori_loop(q * per, (q + 1) * per, sums_body, acc)
-    sums = [jnp.broadcast_to(jnp.sum(a, axis=1, keepdims=True), (NF, 128)) for a in acc]
+    tw = jnp.sum(acc[12], axis=1, keepdims=True)
+    tm = jnp.sum(acc[13], axis=1, keepdims=True) + lc * tw
+    sums = [jnp.broadcast_to(jnp.sum(a, axis=1, keepdims=True), (NF, 128)) for a in acc[:12]]
     wide = [jnp.broadcast_to(lc[i : i + 1], (NF, 128)) for i in range(3)]
     wide_m = [jnp.broadcast_to(tm[i : i + 1], (NF, 128)) for i in range(3)]
     tile = jnp.broadcast_to(tw, (NF, 128))
@@ -247,55 +251,66 @@
     dcopy.wait_recv()
 
     erow = lax.broadcasted_iota(jnp.int32, (16, 2 * FP), 0)
-    ones = [jnp.where(erow == i, 1.0, 0.0).astype(BF16) for i in range(3)]
+    ones = [jnp.where(erow == i, 1.0, 0.0).astype(BF16) for i in range(6)]
+    coef = cpt[:, 0 : 2 * FP]
+    coef2 = [jnp.concatenate([coef, ones[3 * q + 2]], axis=0) for q in range(2)]
 
     def mm(lhs, rhs):
         return jnp.dot(lhs, rhs, preferred_element_type=F32)
 
-    def term_a(dest, h, emit):
-        def body(q, c):
-            blk = dest * NZ + h * (NZ // 2) + q
+    def zblk(g, q):
+        return (pz + PARTS[g][q]) % NZ
+
+    def term_a(dest, g, emit):
+        for q in range(2):
+            blk = dest * NZ + zblk(g, q)
             for i in range(2):
-                emit(q, i, mm(cpt[:, 0 : 2 * FP], dall[blk, i]))
-            return c
-
-        lax.fori_loop(0, NZ // 2, body, 0)
-
-    def term_b(dest, h, emit):
-        def body(q, c):
+                emit(q, i, mm(coef, dall[blk, i]))
+
+    def term_b(dest, h, ref):
+        tail = None
+        for q in range(2):
             blk = (h * (NX // 2) + q) * NZ + dest
-            emit(q, 0, mm(cpt[:, 0 : 2 * FP], dall[blk, 2]))
-            sh = mm(ones[0], dall[blk, 0]) + mm(ones[1], dall[blk, 1]) + mm(ones[2], dall[blk, 2])
-            emit(q, 1, sh)
-            return c
-
-        lax.fori_loop(0, NX // 2, body, 0)
+            t = mm(coef2[q], dall[blk, 2])
+            ref[32 * q : 32 * q + 32, :] = t[0:32].astype(ref.dtype)
+            t = t[32:48] + (mm(ones[3 * q], dall[blk, 0]) + mm(ones[3 * q + 1], dall[blk, 1]))
+            tail = t if tail is None else tail + t
+        ref[64:80, :] = tail.astype(ref.dtype)
 
     def rowslice(i):
         return slice(32 * i, 32 * i + 32)
 
-    def brow(i):
-        return slice(0, 32) if i == 0 else slice(32, 48)
+    def store(ref, rows_of):
+        def emit(q, i, t):
+            ref[q, rows_of(i), :] = t.astype(ref.dtype)
+
+        return emit
 
     class Stage:
-        def __init__(self, length, pos, sbuf, rbuf, ssm, rsm, fill, peer_of, cut):
+        def __init__(self, length, pos, parts, sbuf, rbuf, ssm, rsm, fill, peer_of, cut):
             self.length, self.pos, self.sbuf, self.rbuf = length, pos, sbuf, rbuf
             self.ssm, self.rsm, self.fill, self.peer_of, self.cut = ssm, rsm, fill, peer_of, cut
+            self.streams = tuple((h, d) for h in range(parts) for d in (1, -1))
             self.copies = {}
 
+        def steps(self, st):
+            h, d = self.streams[st]
+            return steps_of(self.length, h % 2, d)
+
+        def dest(self, st, s):
+            h, d = self.streams[st]
+            return (self.pos + (d * (self.steps(st) - s) + self.length)) % self.length
+
         def send(self, st, s):
-            h, d = STREAMS[st]
-            total_steps = steps_of(self.length, h, d)
-            if s >= total_steps:
+            h, d = self.streams[st]
+            if s >= self.steps(st):
                 return
-            dest = (self.pos + (d * (total_steps - s) + self.length)) % self.length
             if s == 0:
                 src = self.sbuf.at[st]
-                self.fill(src, dest, h, False)
             else:
                 self.copies[st, s - 1].wait_recv()
                 src = self.rbuf.at[st, s - 1]
-                self.fill(src, dest, h, True)
+            self.fill(src, st, s)
             c = remote(
                 self.cut(src, h), self.cut(self.rbuf.at[st, s], h), self.ssm.at[st, s], self.rsm.at[st, s],
                 self.peer_of(d),
@@ -306,46 +321,41 @@
 
         def finals(self, h):
             out = []
-            for st, (hh, d) in enumerate(STREAMS):
+            for st, (hh, d) in enumerate(self.streams):
                 if hh == h:
-                    s = steps_of(self.length, h, d) - 1
+                    s = self.steps(st) - 1
                     self.copies[st, s].wait_recv()
                     out.append(self.rbuf.at[st, s])
             return out
 
-    def fill_a1(ref, dest, h, add):
-        def emit(q, i, t):
-            if add:
-                t = t + ref[q, rowslice(i), :].astype(F32)
-            ref[q, rowslice(i), :] = t.astype(BF16)
-
-        term_a(dest, h, emit)
-
-    def fill_b1(ref, dest, h, add):
-        def emit(q, i, t):
-            if add:
-                t = t + ref[q, brow(i), :].astype(F32)
-            ref[q, brow(i), :] = t.astype(BF16)
-
-        term_b(dest, h, emit)
-
-    def fill_a2(ref, dest, h, add):
-        t = acca[dest, rowslice(h), :]
-        if add:
+    def fill_a1(ref, st, s):
+        g = st // 2
+        if s == 0:
+            term_a(sa1.dest(st, 0), g, store(ref, rowslice))
+        else:
+            ref[...] = (taf[g] + ref[...].astype(F32)).astype(BF16)
+
+    def fill_b1(ref, st, s):
+        if s == 0:
+            term_b(sb1.dest(st, 0), st // 2, ref)
+        else:
+            ref[...] = (tbf[st, s - 1] + ref[...].astype(F32)).astype(BF16)
+
+    def fill_a2(ref, st, s):
+        t = acca[sa2.dest(st, s), rowslice(st // 2), :]
+        if s:
             t = t + ref[...].astype(F32)
         ref[...] = t.astype(BF16)
 
-    def fill_b2(ref, dest, h, add):
-        if h == 0:
-            t = accb[dest, 0:32, :]
-            if add:
-                t = t + ref[...].astype(F32)
-            ref[...] = t.astype(BF16)
+    def fill_b2(ref, st, s):
+        e = sb2.dest(st, s)
+        if st // 2 == 0:
+            size, t = 32, accb[e // 2, pl.ds(pl.multiple_of(e % 2 * 32, 32), 32), :]
         else:
-            t = accb[dest, 32:48, :]
-            if add:
-                t = t + ref[0:16, :].astype(F32)
-            ref[0:16, :] = t.astype(BF16)
+            size, t = 16, accb[e // 2, 64:80, :]
+        if s:
+            t = t + ref[0:size, :].astype(F32)
+        ref[0:size, :] = t.astype(BF16)
 
     def whole(ref, h):
         return ref
@@ -355,60 +365,86 @@
 
     x_dir = {1: dev(dx=1), -1: dev(dx=-1)}
     z_dir = {1: dev(dz=1), -1: dev(dz=-1)}
-    sa1 = Stage(NX, px, a1s, a1r, a1ss, a1rs, fill_a1, x_dir.get, whole)
-    sb1 = Stage(NZ, pz, b1s, b1r, b1ss, b1rs, fill_b1, z_dir.get, whole)
-    sa2 = Stage(NZ, pz, a2s, a2r, a2ss, a2rs, fill_a2, z_dir.get, whole)
-    sb2 = Stage(NX, px, b2s, b2r, b2ss, b2rs, fill_b2, x_dir.get, cut_b2)
+    sa1 = Stage(NX, px, 4, a1s, a1r, a1ss, a1rs, fill_a1, x_dir.get, whole)
+    sb1 = Stage(NZ, pz, 2, b1s, b1r, b1ss, b1rs, fill_b1, z_dir.get, whole)
+    sa2 = Stage(NZ, pz, 2, a2s, a2r, a2ss, a2rs, fill_a2, z_dir.get, whole)
+    sb2 = Stage(NX, px, 2, b2s, b2r, b2ss, b2rs, fill_b2, x_dir.get, cut_b2)
 
     order = (0, 3, 2, 1)
     for st in order:
         sa1.send(st, 0)
         sb1.send(st, 0)
-    for st in order:
-        sb1.send(st, 1)
-    for st in order:
-        sa1.send(st, 1)
+    sa1.send(4, 0)
+    sa1.send(7, 0)
+    for s in range(1, NZ // 2):
+        for st in order:
+            if s < sb1.steps(st):
+                term_b(sb1.dest(st, s), st // 2, tbf.at[st, s - 1])
+        if s == 1:
+            term_a(sa1.dest(0, 1), 0, store(taf.at[0], rowslice))
+            term_a(sa1.dest(3, 1), 1, store(taf.at[1], rowslice))
+            for st in order:
+                sb1.send(st, 1)
+            sa1.send(0, 1)
+            sa1.send(3, 1)
+            sa1.send(6, 0)
+            sa1.send(5, 0)
+            term_a(sa1.dest(4, 1), 2, store(taf.at[2], rowslice))
+            term_a(sa1.dest(7, 1), 3, store(taf.at[3], rowslice))
+
+    def own_a(g):
+        def emit(q, i, t):
+            acca[zblk(g, q), rowslice(i), :] = t
+
+        term_a(px, g, emit)
+
+    def fin_a(g):
+        f0, f1 = sa1.finals(g)
+        for q in range(2):
+            z = zblk(g, q)
+            acca[z] = acca[z] + (f0[q].astype(F32) + f1[q].astype(F32))
+
+    own_a(0)
+    own_a(1)
     for st in order:
         sb1.send(st, 2)
+    sa1.send(4, 1)
+    sa1.send(7, 1)
+    own_a(2)
+    own_a(3)
+    for h in (0, 1):
+        term_b(pz, h, accb.at[h])
+    fin_a(0)
+    fin_a(1)
+    for st in order:
+        sa2.send(st, 0)
     for st in order:
         sb1.send(st, 3)
-
-    for h in (0, 1):
-        f0, f1 = sa1.finals(h)
-
-        def emit(q, i, t, f0=f0, f1=f1, h=h):
-            t = t + f0[q, rowslice(i), :].astype(F32) + f1[q, rowslice(i), :].astype(F32)
-            acca[h * (NZ // 2) + q, rowslice(i), :] = t
-
-        term_a(px, h, emit)
-    for st in order:
-        sa2.send(st, 0)
+    for st in (0, 3, 2):
+        sa2.send(st, 1)
     for h in (0, 1):
         f0, f1 = sb1.finals(h)
-
-        def emit(q, i, t, f0=f0, f1=f1, h=h):
-            t = t + f0[q, brow(i), :].astype(F32) + f1[q, brow(i), :].astype(F32)
-            accb[h * (NX // 2) + q, brow(i), :] = t
-
-        term_b(pz, h, emit)
+        accb[h] = accb[h] + (f0[...].astype(F32) + f1[...].astype(F32))
     for st in order:
         sb2.send(st, 0)
-    for st in order:
-        sa2.send(st, 1)
+    fin_a(2)
+    fin_a(3)
+    sa2.send(1, 1)
+    for st in order:
+        sa2.send(st, 2)
     for st in order:
         sb2.send(st, 1)
-    for st in order:
-        sa2.send(st, 2)
     for st in order:
         sa2.send(st, 3)
 
     inv_f = 1.0 / FRAMES
     f0, f1 = sb2.finals(0)
-    img2 = (accb[px, 0:32, :] + f0[...].astype(F32) + f1[...].astype(F32)) * inv_f
+    img2 = (accb[px // 2, pl.ds(pl.multiple_of(px % 2 * 32, 32), 32), :] + f0[...].astype(F32) + f1[...].astype(F32)) * inv_f
     f0, f1 = sb2.finals(1)
-    shift = accb[px, 32:48, :] + f0[0:16, :].astype(F32) + f1[0:16, :].astype(F32)
+    shift = accb[px // 2, 64:80, :] + f0[0:16, :].astype(F32) + f1[0:16, :].astype(F32)
+    shift = jnp.where(px % 2 == 0, shift[0:3], shift[3:6])
     own = pl.ds(pl.multiple_of(n * BLK, 128), BLK)
-    nm_ref[...] = ms_ref[:, own] + shift[0:3] * inv_f
+    nm_ref[...] = ms_ref[:, own] + shift * inv_f
     imgs = []
     for h in (0, 1):
         f0, f1 = sa2.finals(h)
@@ -443,11 +479,18 @@
     v = g_ref[...]
     m = jnp.concatenate([v] + [pltpu.roll(v, 128 - 32 * q, 1) for q in range(1, 4)], axis=0)
     m = jnp.where(lanes < K, m, jnp.where(lanes - K == rows, 1.0, 0.0))
-    for j in range(K - 1):
-        prow = jnp.broadcast_to(m[j : j + 1, :], (K, 128))
-        pcol = jnp.broadcast_to(m[:, j : j + 1], (K, 128))
-        piv = 1.0 / pcol[j : j + 1, :]
-        m = jnp.where(rows > j, m - pcol * (prow * piv), m)
+    for j in range(0, K, 2):
+        r0 = m[j : j + 1, :]
+        r1 = m[j + 1 : j + 2, :]
+        c0 = jnp.broadcast_to(m[:, j : j + 1], (K, 128))
+        c1 = jnp.broadcast_to(m[:, j + 1 : j + 2], (K, 128))
+        ia = 1.0 / c0[j : j + 1, :]
+        ratio = c0[j + 1 : j + 2, :] * ia
+        r1 = r1 - ratio * r0
+        u1 = r1 * (1.0 / (c1[j + 1 : j + 2, :] - ratio * c1[j : j + 1, :]))
+        u0 = (r0 - c1[j : j + 1, :] * u1) * ia
+        nxt = m - (c0 * jnp.broadcast_to(u0, (K, 128)) + c1 * jnp.broadcast_to(u1, (K, 128)))
+        m = jnp.where(rows > j + 1, nxt, jnp.where(rows == j + 1, jnp.broadcast_to(r1, (K, 128)), m))
     diag = jnp.sum(jnp.where(rows == lanes, m, 0.0), axis=1, keepdims=True)
     linv = pltpu.roll(m, 128 - K, 1) * (1.0 / jnp.sqrt(diag))
     linv = linv[:, 0:K]
@@ -465,28 +508,29 @@
     dma = pltpu.SemaphoreType.DMA
     V = pltpu.VMEM
     scratch = [
-        V((3, NF, AL), F32), V((3, K, AL), BF16), V((NB, 3, 2 * FP, BLK), BF16), V((NB, 3, FP, BLK), BF16),
+        V((3, AL), F32), V((1, AL), F32), V((3, NF, AL), F32), V((3, K, AL), BF16), V((NB, 3, 2 * FP, BLK), BF16), V((NB, 3, FP, BLK), BF16),
         V((12, NF, 128), F32), V((NY, NF, 128), F32), V((NY, K, 128), F32), V((2, K, 128), F32), V((K, 128), F32),
         V((NB * NC, 1, 128), F32), V((K, 128), BF16),
         V((NX * NC * NY, 8, 128), F32), V((NZ, 8, 128), F32),
-        V((4, NZ // 2, 64, BLK), BF16), V((4, NX // 2, NZ // 2, 64, BLK), BF16),
-        V((4, NX // 2, 48, BLK), BF16), V((4, NZ // 2, NX // 2, 48, BLK), BF16),
+        V((8, 2, 64, BLK), BF16), V((8, NX // 2, 2, 64, BLK), BF16),
+        V((4, 80, BLK), BF16), V((4, NZ // 2, 80, BLK), BF16),
         V((4, 32, BLK), BF16), V((4, NZ // 2, 32, BLK), BF16),
         V((4, 32, BLK), BF16), V((4, NX // 2, 32, BLK), BF16),
-        V((NZ, 64, BLK), F32), V((NX, 48, BLK), F32),
-        dma((CHUNKS,)), dma,
+        V((NZ, 64, BLK), F32), V((2, 80, BLK), F32),
+        V((4, 2, 64, BLK), F32), V((4, NZ // 2 - 1, 80, BLK), F32),
+        dma, dma, dma((CHUNKS,)), dma,
         dma((NY - 1,)), dma((NY - 1,)), dma((NY - 1,)), dma((NY - 1,)),
         dma((NB * NC - 1,)), dma((NB * NC - 1,)),
         dma, dma, dma, dma,
         dma((NX * NC * NY - 1,)), dma((NX * NC * NY - 1,)), dma((NZ - 1,)), dma((NZ - 1,)),
-        dma((4, NX // 2)), dma((4, NX // 2)), dma((4, NZ // 2)), dma((4, NZ // 2)),
+        dma((8, NX // 2)), dma((8, NX // 2)), dma((4, NZ // 2)), dma((4, NZ // 2)),
         dma((4, NZ // 2)), dma((4, NZ // 2)), dma((4, NX // 2)), dma((4, NX // 2)),
     ]
     shapes = [(3, BLK), (3, K, BLK), (8, 128)]
     nm, img, gram = pl.pallas_call(
         kernel,
         out_shape=tuple(jax.ShapeDtypeStruct(d, F32) for d in shapes),
-        in_specs=[anyspec, vm, vm, anyspec],
+        in_specs=[anyspec] * 4,
         out_specs=(vm, vm, vm),
         scratch_shapes=scratch,
         compiler_params=pltpu.CompilerParams(

time: 79.9 us -> 73.5 us (0.920)
  Pallas kernels: 79.2 us -> 72.7 us
    pallas_call x1, Pallas kernels: 74.7 us -> 69.1 us  [per_device(): pl.pallas_call(kernel, out_shape=tuple((jax.ShapeDtypeStruct(d, F32) for...]
    pallas_call x1, Pallas kernels: 4.47 us -> 3.59 us  [per_device(): pl.pallas_call(finish, out_shape=tuple((jax.ShapeDtypeStruct(d, F32) for...]
where the time goes in v3:
time: 73.5 us; the launch traced here: 73.4 us
  Pallas kernels  72.7 us (99%)
    pallas_call x1, Pallas kernels, per_device(): pl.pallas_call(kernel, out_shape=tuple((jax.ShapeDtypeStruct(d, F32) for...  69.1 us
    pallas_call x1, Pallas kernels, per_device(): pl.pallas_call(finish, out_shape=tuple((jax.ShapeDtypeStruct(d, F32) for...  3.59 us

profile of v3, /device:TPU:1, one launch (start us, length us, event | category | flops | bytes accessed | tf_op | source)
XLA Modules:
  0.0 73.4 jit_solution(2789809941809349633)
XLA Ops:
  0.6 69.1 %shard_map.67 = (f32[3,384]{1,0:T(4,128)}, f32[3,32,384]{2,1,0:T(8,128)}, f32[8,128]{1,0:T(8,128)}) custom-call(f32[3,24,24576]{2,1,0:T(8,128)} %bitcast.5, f32[3,24576]{1,0:T(4,128)} %ms_hbm.1, f32[1,24576]{1,0:T(1,128)} %bitcast.7, bf16[3,32,24576]{2,1,0:T(8,128)(2,1)} %bitcast.6), custom_call_target="tpu_custom_call" | custom-call | tf_op jit(solution)/shard_map/pallas_call | solution.py:530
  69.8 3.6 %shard_map.68 = (f32[3,384]{1,0:T(4,128)}, f32[3,32,384]{2,1,0:T(8,128)}, f32[3,32,384]{2,1,0:T(8,128)}) custom-call(f32[3,384]{1,0:T(4,128)} %get-tuple-element.9.nm_in, f32[3,32,384]{2,1,0:T(8,128)} %get-tuple-element.10.img_in, f32[8,128]{1,0:T(8,128)} %get-tuple-element.11.g_ref), custom_call_target="tpu_custom_call" | custom-call | tf_op jit(solution)/shard_map/pallas_call | solution.py:541

commit v4 on v3

--- a/solution.py
+++ b/solution.py
@@ -18,7 +18,7 @@
 CHUNKS = 8
 CW = AL // CHUNKS
 STEP = 512
-UNROLL = 8
+UNROLL = 16
 VLHS = False
 F32 = jnp.float32
 BF16 = jnp.bfloat16
@@ -60,9 +60,9 @@
 def kernel(
     x_hbm, ms_hbm, w_hbm, s_hbm, nm_ref, img_ref, g_ref,
     ms_ref, w_ref, xv, sv, dall, dsend, rot, ex1, ex2, pp, gsq, pba, cpt, gx, gz,
-    a1s, a1r, b1s, b1r, a2s, a2r, b2s, b2r, acca, accb, taf, tbf,
+    a1s, a1r, b1s, b1r, a2s, a2r, h4s, h4r, b2s, b2r, acca, accb, taf, tbf,
     msem, wsem, xsem, ssem, y1s, y1r, y2s, y2r, px_s, px_r, pp_s, pp_r, dx_s, dx_r,
-    gx_s, gx_r, gz_s, gz_r, a1ss, a1rs, b1ss, b1rs, a2ss, a2rs, b2ss, b2rs,
+    gx_s, gx_r, gz_s, gz_r, a1ss, a1rs, b1ss, b1rs, a2ss, a2rs, h4ss, h4rs, b2ss, b2rs,
 ):
     y = lax.axis_index("atoms")
     n = lax.axis_index("frames")
@@ -287,11 +287,12 @@
         return emit
 
     class Stage:
-        def __init__(self, length, pos, parts, sbuf, rbuf, ssm, rsm, fill, peer_of, cut):
+        def __init__(self, length, pos, parts, sbuf, rbuf, ssm, rsm, fill, peer_of, subs):
             self.length, self.pos, self.sbuf, self.rbuf = length, pos, sbuf, rbuf
-            self.ssm, self.rsm, self.fill, self.peer_of, self.cut = ssm, rsm, fill, peer_of, cut
+            self.ssm, self.rsm, self.fill, self.peer_of, self.subs = ssm, rsm, fill, peer_of, subs
             self.streams = tuple((h, d) for h in range(parts) for d in (1, -1))
             self.copies = {}
+            self.filled = set()
 
         def steps(self, st):
             h, d = self.streams[st]
@@ -300,6 +301,10 @@
         def dest(self, st, s):
             h, d = self.streams[st]
             return (self.pos + (d * (self.steps(st) - s) + self.length)) % self.length
+
+        def prepare(self, st):
+            self.fill(self.sbuf.at[st], st, 0, None)
+            self.filled.add(st)
 
         def send(self, st, s):
             h, d = self.streams[st]
@@ -307,90 +312,79 @@
                 return
             if s == 0:
                 src = self.sbuf.at[st]
+                if st not in self.filled:
+                    self.prepare(st)
             else:
-                self.copies[st, s - 1].wait_recv()
                 src = self.rbuf.at[st, s - 1]
-            self.fill(src, st, s)
-            c = remote(
-                self.cut(src, h), self.cut(self.rbuf.at[st, s], h), self.ssm.at[st, s], self.rsm.at[st, s],
-                self.peer_of(d),
-            )
-            c.start()
-            pending.append(c)
-            self.copies[st, s] = c
+            for k, sub in enumerate(self.subs):
+                if s:
+                    self.copies[st, s - 1, k].wait_recv()
+                    self.fill(src.at[sub], st, s, sub)
+                c = remote(
+                    src.at[sub], self.rbuf.at[st, s].at[sub], self.ssm.at[st, s, k], self.rsm.at[st, s, k],
+                    self.peer_of(d),
+                )
+                c.start()
+                pending.append(c)
+                self.copies[st, s, k] = c
 
         def finals(self, h):
             out = []
             for st, (hh, d) in enumerate(self.streams):
                 if hh == h:
                     s = self.steps(st) - 1
-                    self.copies[st, s].wait_recv()
+                    for k in range(len(self.subs)):
+                        self.copies[st, s, k].wait_recv()
                     out.append(self.rbuf.at[st, s])
             return out
 
-    def fill_a1(ref, st, s):
+    def fill_a1(ref, st, s, sub):
         g = st // 2
         if s == 0:
             term_a(sa1.dest(st, 0), g, store(ref, rowslice))
         else:
             ref[...] = (taf[g] + ref[...].astype(F32)).astype(BF16)
 
-    def fill_b1(ref, st, s):
+    def fill_b1(ref, st, s, sub):
         if s == 0:
             term_b(sb1.dest(st, 0), st // 2, ref)
         else:
-            ref[...] = (tbf[st, s - 1] + ref[...].astype(F32)).astype(BF16)
-
-    def fill_a2(ref, st, s):
-        t = acca[sa2.dest(st, s), rowslice(st // 2), :]
-        if s:
-            t = t + ref[...].astype(F32)
-        ref[...] = t.astype(BF16)
-
-    def fill_b2(ref, st, s):
-        e = sb2.dest(st, s)
-        if st // 2 == 0:
-            size, t = 32, accb[e // 2, pl.ds(pl.multiple_of(e % 2 * 32, 32), 32), :]
-        else:
-            size, t = 16, accb[e // 2, 64:80, :]
-        if s:
-            t = t + ref[0:size, :].astype(F32)
-        ref[0:size, :] = t.astype(BF16)
-
-    def whole(ref, h):
-        return ref
-
-    def cut_b2(ref, h):
-        return ref if h == 0 else ref.at[0:16, :]
+            ref[...] = (tbf[st, s - 1, sub] + ref[...].astype(F32)).astype(BF16)
 
     x_dir = {1: dev(dx=1), -1: dev(dx=-1)}
     z_dir = {1: dev(dz=1), -1: dev(dz=-1)}
-    sa1 = Stage(NX, px, 4, a1s, a1r, a1ss, a1rs, fill_a1, x_dir.get, whole)
-    sb1 = Stage(NZ, pz, 2, b1s, b1r, b1ss, b1rs, fill_b1, z_dir.get, whole)
-    sa2 = Stage(NZ, pz, 2, a2s, a2r, a2ss, a2rs, fill_a2, z_dir.get, whole)
-    sb2 = Stage(NX, px, 2, b2s, b2r, b2ss, b2rs, fill_b2, x_dir.get, cut_b2)
+    sa1 = Stage(NX, px, 4, a1s, a1r, a1ss, a1rs, fill_a1, x_dir.get, (slice(0, 2),))
+    sb1 = Stage(NZ, pz, 2, b1s, b1r, b1ss, b1rs, fill_b1, z_dir.get, (slice(0, 32), slice(32, 80)))
 
     order = (0, 3, 2, 1)
     for st in order:
         sa1.send(st, 0)
         sb1.send(st, 0)
-    sa1.send(4, 0)
-    sa1.send(7, 0)
-    for s in range(1, NZ // 2):
+
+    def terms_b(s):
         for st in order:
             if s < sb1.steps(st):
                 term_b(sb1.dest(st, s), st // 2, tbf.at[st, s - 1])
-        if s == 1:
-            term_a(sa1.dest(0, 1), 0, store(taf.at[0], rowslice))
-            term_a(sa1.dest(3, 1), 1, store(taf.at[1], rowslice))
-            for st in order:
-                sb1.send(st, 1)
-            sa1.send(0, 1)
-            sa1.send(3, 1)
-            sa1.send(6, 0)
-            sa1.send(5, 0)
-            term_a(sa1.dest(4, 1), 2, store(taf.at[2], rowslice))
-            term_a(sa1.dest(7, 1), 3, store(taf.at[3], rowslice))
+
+    def terms_a(st):
+        term_a(sa1.dest(st, 1), st // 2, store(taf.at[st // 2], rowslice))
+
+    terms_a(0)
+    terms_a(3)
+    terms_b(1)
+    for st in (4, 7, 6, 5):
+        sa1.prepare(st)
+    for st in (0, 3):
+        sb1.send(st, 1)
+        sa1.send(st, 1)
+    for st in (4, 7, 6, 5):
+        sa1.send(st, 0)
+    for st in (2, 1):
+        sb1.send(st, 1)
+    terms_b(2)
+    terms_b(3)
+    terms_a(4)
+    terms_a(7)
 
     def own_a(g):
         def emit(q, i, t):
@@ -408,47 +402,76 @@
     own_a(1)
     for st in order:
         sb1.send(st, 2)
-    sa1.send(4, 1)
-    sa1.send(7, 1)
+
+    second = {}
+
+    def straight(key, src, dst, ssm, rsm, peer):
+        c = remote(src, dst, ssm, rsm, peer)
+        c.start()
+        pending.append(c)
+        second[key] = c
+
+    def send_z(r, merged=None):
+        t = acca[(pz + r) % NZ]
+        if merged is None:
+            a2s[r] = t.astype(BF16)
+        else:
+            half = rowslice(merged)
+            second["h", merged].wait_recv()
+            a2s[r] = t.astype(BF16)
+            a2s[r, half, :] = (acca[(pz + r) % NZ, half, :] + h4r[merged].astype(F32)).astype(BF16)
+        straight(("z", r), a2s.at[r], a2r.at[r], a2ss.at[r], a2rs.at[r], z_peers[r - 1])
+
+    fin_a(0)
+    fin_a(1)
+    for h, d in ((0, 1), (1, -1)):
+        h4s[h] = acca[(pz + 4) % NZ, rowslice(h), :].astype(BF16)
+        straight(("h", h), h4s.at[h], h4r.at[h], h4ss.at[h], h4rs.at[h], z_dir[d])
+    send_z(2)
     own_a(2)
     own_a(3)
     for h in (0, 1):
         term_b(pz, h, accb.at[h])
-    fin_a(0)
-    fin_a(1)
-    for st in order:
-        sa2.send(st, 0)
+    sa1.send(4, 1)
+    sa1.send(7, 1)
     for st in order:
         sb1.send(st, 3)
-    for st in (0, 3, 2):
-        sa2.send(st, 1)
+    send_z(3, 0)
+    send_z(5, 1)
+    fin_a(2)
+    fin_a(3)
+    for r in (6, 1, 7):
+        send_z(r)
     for h in (0, 1):
         f0, f1 = sb1.finals(h)
         accb[h] = accb[h] + (f0[...].astype(F32) + f1[...].astype(F32))
-    for st in order:
-        sb2.send(st, 0)
-    fin_a(2)
-    fin_a(3)
-    sa2.send(1, 1)
-    for st in order:
-        sa2.send(st, 2)
-    for st in order:
-        sb2.send(st, 1)
-    for st in order:
-        sa2.send(st, 3)
+
+    def own_b(e):
+        return accb[e // 2, pl.ds(pl.multiple_of(e % 2 * 32, 32), 32), :]
+
+    for d in (2, 1, 3):
+        e = (px + d) % NX
+        b2s[d, 0:32, :] = own_b(e).astype(BF16)
+        b2s[d, 32:48, :] = accb[e // 2, 64:80, :].astype(BF16)
+        straight(("x", d), b2s.at[d], b2r.at[d], b2ss.at[d], b2rs.at[d], dev(dx=d))
 
     inv_f = 1.0 / FRAMES
-    f0, f1 = sb2.finals(0)
-    img2 = (accb[px // 2, pl.ds(pl.multiple_of(px % 2 * 32, 32), 32), :] + f0[...].astype(F32) + f1[...].astype(F32)) * inv_f
-    f0, f1 = sb2.finals(1)
-    shift = accb[px // 2, 64:80, :] + f0[0:16, :].astype(F32) + f1[0:16, :].astype(F32)
+    whole = acca[pz]
+    for r in (2, 3, 5, 6, 1, 7):
+        second["z", r].wait_recv()
+        whole = whole + a2r[r].astype(F32)
+    whole = whole * inv_f
+    img2 = own_b(px)
+    shift = accb[px // 2, 64:80, :]
+    for d in (2, 1, 3):
+        second["x", d].wait_recv()
+        img2 = img2 + b2r[d, 0:32, :].astype(F32)
+        shift = shift + b2r[d, 32:48, :].astype(F32)
+    img2 = img2 * inv_f
     shift = jnp.where(px % 2 == 0, shift[0:3], shift[3:6])
     own = pl.ds(pl.multiple_of(n * BLK, 128), BLK)
     nm_ref[...] = ms_ref[:, own] + shift * inv_f
-    imgs = []
-    for h in (0, 1):
-        f0, f1 = sa2.finals(h)
-        imgs.append((acca[pz, rowslice(h), :] + f0[...].astype(F32) + f1[...].astype(F32)) * inv_f)
+    imgs = [whole[0:32], whole[32:64]]
     imgs.append(img2)
     g = None
     for i in range(3):
@@ -514,8 +537,8 @@
         V((NX * NC * NY, 8, 128), F32), V((NZ, 8, 128), F32),
         V((8, 2, 64, BLK), BF16), V((8, NX // 2, 2, 64, BLK), BF16),
         V((4, 80, BLK), BF16), V((4, NZ // 2, 80, BLK), BF16),
-        V((4, 32, BLK), BF16), V((4, NZ // 2, 32, BLK), BF16),
-        V((4, 32, BLK), BF16), V((4, NX // 2, 32, BLK), BF16),
+        V((NZ, 64, BLK), BF16), V((NZ, 64, BLK), BF16), V((2, 32, BLK), BF16), V((2, 32, BLK), BF16),
+        V((NX, 48, BLK), BF16), V((NX, 48, BLK), BF16),
         V((NZ, 64, BLK), F32), V((2, 80, BLK), F32),
         V((4, 2, 64, BLK), F32), V((4, NZ // 2 - 1, 80, BLK), F32),
         dma, dma, dma((CHUNKS,)), dma,
@@ -523,8 +546,8 @@
         dma((NB * NC - 1,)), dma((NB * NC - 1,)),
         dma, dma, dma, dma,
         dma((NX * NC * NY - 1,)), dma((NX * NC * NY - 1,)), dma((NZ - 1,)), dma((NZ - 1,)),
-        dma((8, NX // 2)), dma((8, NX // 2)), dma((4, NZ // 2)), dma((4, NZ // 2)),
-        dma((4, NZ // 2)), dma((4, NZ // 2)), dma((4, NX // 2)), dma((4, NX // 2)),
+        dma((8, NX // 2, 1)), dma((8, NX // 2, 1)), dma((4, NZ // 2, 2)), dma((4, NZ // 2, 2)),
+        dma((NZ,)), dma((NZ,)), dma((2,)), dma((2,)), dma((NX,)), dma((NX,)),
     ]
     shapes = [(3, BLK), (3, K, BLK), (8, 128)]
     nm, img, gram = pl.pallas_call(

time: 73.5 us -> 71 us (0.966)
  Pallas kernels: 72.7 us -> 70.2 us
    pallas_call x1, Pallas kernels: 69.1 us -> 66.6 us  [per_device(): pl.pallas_call(kernel, out_shape=tuple((jax.ShapeDtypeStruct(d, F32) for...]
where the time goes in v4:
time: 71 us; the launch traced here: 70.9 us
  Pallas kernels  70.2 us (99%)
    pallas_call x1, Pallas kernels, per_device(): pl.pallas_call(kernel, out_shape=tuple((jax.ShapeDtypeStruct(d, F32) for...  66.6 us
    pallas_call x1, Pallas kernels, per_device(): pl.pallas_call(finish, out_shape=tuple((jax.ShapeDtypeStruct(d, F32) for...  3.59 us

profile of v4, /device:TPU:1, one launch (start us, length us, event | category | flops | bytes accessed | tf_op | source)
XLA Modules:
  0.0 70.9 jit_solution(3575419116486972944)
XLA Ops:
  0.6 66.6 %shard_map.67 = (f32[3,384]{1,0:T(4,128)}, f32[3,32,384]{2,1,0:T(8,128)}, f32[8,128]{1,0:T(8,128)}) custom-call(f32[3,24,24576]{2,1,0:T(8,128)} %bitcast.5, f32[3,24576]{1,0:T(4,128)} %ms_hbm.1, f32[1,24576]{1,0:T(1,128)} %bitcast.7, bf16[3,32,24576]{2,1,0:T(8,128)(2,1)} %bitcast.6), custom_call_target="tpu_custom_call" | custom-call | tf_op jit(solution)/shard_map/pallas_call | solution.py:553
  67.3 3.6 %shard_map.68 = (f32[3,384]{1,0:T(4,128)}, f32[3,32,384]{2,1,0:T(8,128)}, f32[3,32,384]{2,1,0:T(8,128)}) custom-call(f32[3,384]{1,0:T(4,128)} %get-tuple-element.9.nm_in, f32[3,32,384]{2,1,0:T(8,128)} %get-tuple-element.10.img_in, f32[8,128]{1,0:T(8,128)} %get-tuple-element.11.g_ref), custom_call_target="tpu_custom_call" | custom-call | tf_op jit(solution)/shard_map/pallas_call | solution.py:564

commit v5 on v4

--- a/solution.py
+++ b/solution.py
@@ -17,7 +17,7 @@
 NB = NX * NZ
 CHUNKS = 8
 CW = AL // CHUNKS
-STEP = 512
+STEP = 1024
 UNROLL = 16
 VLHS = False
 F32 = jnp.float32
@@ -162,26 +162,30 @@
         for j in range(3):
             e = 3 * i + j
             tile = jnp.where(lane == e, sums[3 + e], tile)
-            tile = jnp.where(lane == 16 + e, sums[j], tile)
-            tile = jnp.where(lane == 32 + e, wide[i], tile)
-            tile = jnp.where(lane == 48 + e, wide_m[i], tile)
-    ex1[0] = tile
+            tile = jnp.where(lane == 9 + e, sums[j], tile)
+            tile = jnp.where(lane == 18 + e, wide[i], tile)
+            tile = jnp.where(lane == 27 + e, wide_m[i], tile)
+    tile = jnp.where(lane < 42, tile, 0.0)
+    ex1[0] = tile[0:8] + pltpu.roll(tile[8:16], 42, 1) + pltpu.roll(tile[16:24], 84, 1)
     pl.semaphore_wait(barrier, len(greet))
     exchange(ex1, y_peers, y1s, y1r)
 
-    slots = [ex1[j] for j in range(NY)]
+    slots = []
+    for j in range(NY):
+        v = ex1[j]
+        slots.append(jnp.concatenate([v, pltpu.roll(v, 128 - 42, 1), pltpu.roll(v, 128 - 84, 1)], axis=0))
     tsum = slots[0] + slots[1] + slots[2] + slots[3]
-    inv_total = 1.0 / jnp.broadcast_to(tsum[:, 127:128], (NF, 128))
+    inv_total = 1.0 / jnp.broadcast_to(tsum[:, 36:37], (NF, 128))
     tsum = tsum * inv_total
-    mrep = pltpu.roll(tsum, 128 - 48, 1)
+    mrep = pltpu.roll(tsum, 128 - 27, 1)
     packed = None
     for p in slots:
-        t = p + (pltpu.roll(p, 128 - 32, 1) - mrep) * pltpu.roll(p, 128 - 16, 1)
+        t = p + (pltpu.roll(p, 128 - 18, 1) - mrep) * pltpu.roll(p, 128 - 9, 1)
         packed = t if packed is None else packed + t
     packed = packed * inv_total
     r = newton([jnp.broadcast_to(packed[:, q : q + 1], (NF, 128)) for q in range(9)])
-    fc = [jnp.broadcast_to(tsum[:, 16 + j : 17 + j], (NF, 128)) for j in range(3)]
-    mc = [jnp.broadcast_to(tsum[:, 48 + 3 * i : 49 + 3 * i], (NF, 128)) for i in range(3)]
+    fc = [jnp.broadcast_to(tsum[:, 9 + j : 10 + j], (NF, 128)) for j in range(3)]
+    mc = [jnp.broadcast_to(tsum[:, 27 + 3 * i : 28 + 3 * i], (NF, 128)) for i in range(3)]
     for q in range(9):
         rot[q] = r[q]
     for i in range(3):
@@ -229,15 +233,21 @@
     if VLHS:
         pacc = pacc.T
 
-    ex2[0] = jnp.zeros((K, 128), F32)
-    ex2[0, :, 0:FP] = pacc
+    rows = lax.broadcasted_iota(jnp.int32, (K, 128), 0)
+    lanes = lax.broadcasted_iota(jnp.int32, (K, 128), 1)
+    gsq[...] = jnp.zeros((K, 128), F32)
+    gsq[:, 0:FP] = pacc
+    v = gsq[0:8, :]
+    for q in range(1, 4):
+        v = v + pltpu.roll(gsq[8 * q : 8 * q + 8, :], 32 * q, 1)
+    ex2[0] = v
     exchange(ex2, y_peers, y2s, y2r)
-    ptot = ex2[0] + ex2[1] + ex2[2] + ex2[3]
+    v = ex2[0] + ex2[1] + ex2[2] + ex2[3]
+    ptot = jnp.concatenate([v] + [pltpu.roll(v, 128 - 32 * q, 1) for q in range(1, 4)], axis=0)
+    ptot = jnp.where(lanes < FP, ptot, 0.0)
     pp[0] = ptot
     pcopy = remote(pp.at[0], pp.at[1], pp_s, pp_r, partner)
     pcopy.start()
-    rows = lax.broadcasted_iota(jnp.int32, (K, 128), 0)
-    lanes = lax.broadcasted_iota(jnp.int32, (K, 128), 1)
     col = jnp.broadcast_to(jnp.sum(ptot, axis=1, keepdims=True), (K, 128))
     row = jnp.sum(jnp.where(rows == lanes, col, 0.0), axis=0, keepdims=True)
     pba[0] = row
@@ -427,7 +437,6 @@
     for h, d in ((0, 1), (1, -1)):
         h4s[h] = acca[(pz + 4) % NZ, rowslice(h), :].astype(BF16)
         straight(("h", h), h4s.at[h], h4r.at[h], h4ss.at[h], h4rs.at[h], z_dir[d])
-    send_z(2)
     own_a(2)
     own_a(3)
     for h in (0, 1):
@@ -438,6 +447,7 @@
         sb1.send(st, 3)
     send_z(3, 0)
     send_z(5, 1)
+    send_z(2)
     fin_a(2)
     fin_a(3)
     for r in (6, 1, 7):
@@ -532,7 +542,7 @@
     V = pltpu.VMEM
     scratch = [
         V((3, AL), F32), V((1, AL), F32), V((3, NF, AL), F32), V((3, K, AL), BF16), V((NB, 3, 2 * FP, BLK), BF16), V((NB, 3, FP, BLK), BF16),
-        V((12, NF, 128), F32), V((NY, NF, 128), F32), V((NY, K, 128), F32), V((2, K, 128), F32), V((K, 128), F32),
+        V((12, NF, 128), F32), V((NY, 8, 128), F32), V((NY, 8, 128), F32), V((2, K, 128), F32), V((K, 128), F32),
         V((NB * NC, 1, 128), F32), V((K, 128), BF16),
         V((NX * NC * NY, 8, 128), F32), V((NZ, 8, 128), F32),
         V((8, 2, 64, BLK), BF16), V((8, NX // 2, 2, 64, BLK), BF16),

time: 71 us -> 70.5 us (level)
  no operation moved by 1% of the time
where the time goes in v5:
time: 70.5 us; the launch traced here: 70.4 us
  Pallas kernels  69.7 us (99%)
    pallas_call x1, Pallas kernels, per_device(): pl.pallas_call(kernel, out_shape=tuple((jax.ShapeDtypeStruct(d, F32) for...  66.1 us
    pallas_call x1, Pallas kernels, per_device(): pl.pallas_call(finish, out_shape=tuple((jax.ShapeDtypeStruct(d, F32) for...  3.59 us

profile of v5, /device:TPU:1, one launch (start us, length us, event | category | flops | bytes accessed | tf_op | source)
XLA Modules:
  0.0 70.4 jit_solution(13564344319157285452)
XLA Ops:
  0.6 66.1 %shard_map.67 = (f32[3,384]{1,0:T(4,128)}, f32[3,32,384]{2,1,0:T(8,128)}, f32[8,128]{1,0:T(8,128)}) custom-call(f32[3,24,24576]{2,1,0:T(8,128)} %bitcast.5, f32[3,24576]{1,0:T(4,128)} %ms_hbm.1, f32[1,24576]{1,0:T(1,128)} %bitcast.7, bf16[3,32,24576]{2,1,0:T(8,128)(2,1)} %bitcast.6), custom_call_target="tpu_custom_call" | custom-call | tf_op jit(solution)/shard_map/pallas_call | solution.py:563
  66.8 3.6 %shard_map.68 = (f32[3,384]{1,0:T(4,128)}, f32[3,32,384]{2,1,0:T(8,128)}, f32[3,32,384]{2,1,0:T(8,128)}) custom-call(f32[3,384]{1,0:T(4,128)} %get-tuple-element.9.nm_in, f32[3,32,384]{2,1,0:T(8,128)} %get-tuple-element.10.img_in, f32[8,128]{1,0:T(8,128)} %get-tuple-element.11.g_ref), custom_call_target="tpu_custom_call" | custom-call | tf_op jit(solution)/shard_map/pallas_call | solution.py:574

commit v6 on v5

--- a/solution.py
+++ b/solution.py
@@ -76,10 +76,21 @@
         tc = (pc + dc) % NC
         return ((y + dy) % NY, (tx * NZ + tz) * NC + tc)
 
-    y_peers = [dev(dy=j) for j in range(1, NY)]
-    f_peers = [dev(dx=j // (NZ * NC), dz=(j // NC) % NZ, dc=j % NC) for j in range(1, NB * NC)]
-    p_peers = [dev(dy=j // (NX * NC), dx=(j // NC) % NX, dc=j % NC) for j in range(1, NX * NC * NY)]
-    greet = f_peers + [p_peers[j - 1] for j in range(NX * NC, NX * NC * NY)]
+    def hops(o):
+        return sum(min(k, size - k) for k, size in zip(o, (NX, NY, NZ)))
+
+    def peers(nx, ny, nz, nc):
+        offsets = [
+            (a, b, c, e) for a in range(nx) for b in range(ny) for c in range(nz) for e in range(nc) if a + b + c + e
+        ]
+        offsets.sort(key=lambda o: -hops(o))
+        return [dev(dx=a, dy=b, dz=c, dc=e) for a, b, c, e in offsets]
+
+    y_peers = peers(1, NY, 1, 1)
+    f_peers = peers(NX, 1, NZ, NC)
+    p_peers = peers(NX, NY, 1, NC)
+    z_far = peers(1, 1, NZ, 1)
+    greet = f_peers + [dev(dx=a, dy=b, dc=e) for a in range(NX) for b in range(1, NY) for e in range(NC)]
     z_peers = [dev(dz=j) for j in range(1, NZ)]
     partner = dev(dc=1)
 
@@ -496,7 +507,7 @@
     gx[0] = v
     exchange(gx, p_peers, gx_s, gx_r)
     gz[0] = jnp.sum(gx[...], axis=0)
-    exchange(gz, z_peers, gz_s, gz_r)
+    exchange(gz, z_far, gz_s, gz_r)
     v = gz[0]
     for j in range(1, NZ):
         v = v + gz[j]

time: 70.5 us -> 69.1 us (0.980)
  Pallas kernels: 69.7 us -> 68.3 us
    pallas_call x1, Pallas kernels: 66.1 us -> 64.7 us  [per_device(): pl.pallas_call(kernel, out_shape=tuple((jax.ShapeDtypeStruct(d, F32) for...]
where the time goes in v6:
time: 69.1 us; the launch traced here: 69 us
  Pallas kernels  68.3 us (99%)
    pallas_call x1, Pallas kernels, per_device(): pl.pallas_call(kernel, out_shape=tuple((jax.ShapeDtypeStruct(d, F32) for...  64.7 us
    pallas_call x1, Pallas kernels, per_device(): pl.pallas_call(finish, out_shape=tuple((jax.ShapeDtypeStruct(d, F32) for...  3.59 us

profile of v6, /device:TPU:1, one launch (start us, length us, event | category | flops | bytes accessed | tf_op | source)
XLA Modules:
  0.0 69.0 jit_solution(14764717590775005065)
XLA Ops:
  0.6 64.7 %shard_map.67 = (f32[3,384]{1,0:T(4,128)}, f32[3,32,384]{2,1,0:T(8,128)}, f32[8,128]{1,0:T(8,128)}) custom-call(f32[3,24,24576]{2,1,0:T(8,128)} %bitcast.5, f32[3,24576]{1,0:T(4,128)} %ms_hbm.1, f32[1,24576]{1,0:T(1,128)} %bitcast.7, bf16[3,32,24576]{2,1,0:T(8,128)(2,1)} %bitcast.6), custom_call_target="tpu_custom_call" | custom-call | tf_op jit(solution)/shard_map/pallas_call | solution.py:574
  65.4 3.6 %shard_map.68 = (f32[3,384]{1,0:T(4,128)}, f32[3,32,384]{2,1,0:T(8,128)}, f32[3,32,384]{2,1,0:T(8,128)}) custom-call(f32[3,384]{1,0:T(4,128)} %get-tuple-element.9.nm_in, f32[3,32,384]{2,1,0:T(8,128)} %get-tuple-element.10.img_in, f32[8,128]{1,0:T(8,128)} %get-tuple-element.11.g_ref), custom_call_target="tpu_custom_call" | custom-call | tf_op jit(solution)/shard_map/pallas_call | solution.py:585

commit v7 on v6

--- a/solution.py
+++ b/solution.py
@@ -142,9 +142,10 @@
         cols = pl.ds(pl.multiple_of(q * STEP, STEP), STEP)
         wv = w_ref[:, cols]
         wm = (ms_ref[:, cols] - lc) * wv
-        acc[12:] = [tw + wv, tm + wm]
         for t in range(STEP // 128):
             lo = t * 128
+            tw = tw + wv[:, lo : lo + 128]
+            tm = tm + wm[:, lo : lo + 128]
             sub = pl.ds(pl.multiple_of(q * STEP + lo, 128), 128)
             wt = jnp.broadcast_to(wv[:, lo : lo + 128], (NF, 128))
             mt = [jnp.broadcast_to(wm[i : i + 1, lo : lo + 128], (NF, 128)) for i in range(3)]
@@ -153,10 +154,11 @@
                 acc[j] = acc[j] + xj * wt
                 for i in range(3):
                     acc[3 + i * 3 + j] = acc[3 + i * 3 + j] + xj * mt[i]
+        acc[12:] = [tw, tm]
         return tuple(acc)
 
     acc = tuple(jnp.zeros((NF, 128), F32) for _ in range(12))
-    acc += (jnp.zeros((1, STEP), F32), jnp.zeros((3, STEP), F32))
+    acc += (jnp.zeros((1, 128), F32), jnp.zeros((3, 128), F32))
     per = CW // STEP
     for q in range(CHUNKS):
         if q == CHUNKS - 1:

time: 69.1 us -> 68.9 us (level)
  no operation moved by 1% of the time
where the time goes in v7:
time: 68.9 us; the launch traced here: 68.8 us
  Pallas kernels  68.2 us (99%)
    pallas_call x1, Pallas kernels, per_device(): pl.pallas_call(kernel, out_shape=tuple((jax.ShapeDtypeStruct(d, F32) for...  64.6 us
    pallas_call x1, Pallas kernels, per_device(): pl.pallas_call(finish, out_shape=tuple((jax.ShapeDtypeStruct(d, F32) for...  3.59 us

profile of v7, /device:TPU:1, one launch (start us, length us, event | category | flops | bytes accessed | tf_op | source)
XLA Modules:
  0.0 68.8 jit_solution(3878679956185921290)
XLA Ops:
  0.6 64.6 %shard_map.67 = (f32[3,384]{1,0:T(4,128)}, f32[3,32,384]{2,1,0:T(8,128)}, f32[8,128]{1,0:T(8,128)}) custom-call(f32[3,24,24576]{2,1,0:T(8,128)} %bitcast.5, f32[3,24576]{1,0:T(4,128)} %ms_hbm.1, f32[1,24576]{1,0:T(1,128)} %bitcast.7, bf16[3,32,24576]{2,1,0:T(8,128)(2,1)} %bitcast.6), custom_call_target="tpu_custom_call" | custom-call | tf_op jit(solution)/shard_map/pallas_call | solution.py:576
  65.2 3.6 %shard_map.68 = (f32[3,384]{1,0:T(4,128)}, f32[3,32,384]{2,1,0:T(8,128)}, f32[3,32,384]{2,1,0:T(8,128)}) custom-call(f32[3,384]{1,0:T(4,128)} %get-tuple-element.9.nm_in, f32[3,32,384]{2,1,0:T(8,128)} %get-tuple-element.10.img_in, f32[8,128]{1,0:T(8,128)} %get-tuple-element.11.g_ref), custom_call_target="tpu_custom_call" | custom-call | tf_op jit(solution)/shard_map/pallas_call | solution.py:587
